TPU v7x, 512 devices: a whole 4x8x8 slice. The times are simulated.
512 devices in a mesh: cluster: 16 (over z, x_lo), sub: 32 (over y, x_hi, core).
Axes of the slice: x: 4 (x_hi: 2, x_lo: 2; x = x_hi * 2 + x_lo), y: 8, z: 8, core: 2. Of those that a mesh axis runs over, the one named last changes fastest.
Arguments:
- schur_block: bfloat16 [16, 32, 1024, 1024], P('cluster', 'sub'), as said below
- load_cases: float32 [16, 32, 1024, 64], P('cluster', 'sub'), may hold values from -30 to 30
- precond_scale: float32 [16, 32, 1024], P('cluster', 'sub'), may hold values from 0.5 to 2
- coarse_basis: float32 [16, 32, 6, 1024], P('cluster', 'sub'), may hold values from -1 to 1
- coarse_inverse: float32 [16, 192, 192], P('cluster', 'sub'), as said below
- corner_weight: float32 [16, 512], P('cluster', 'sub'), may hold values from 0.5 to 4
- corner_index: int32 [16, 32, 64], P('cluster', 'sub'), may hold values from 0 to 511
- iface_block: int32 [16, 32, 2], P('cluster', 'sub'), may hold values from 0 to 6
- glue_link: int32 [16, 32], P('cluster', 'sub'), may hold values 0 or 1
Outputs:
- solution: float32 [16, 32, 1024, 64], P('cluster', 'sub')
Inputs may be any that keep to these rules, and one draw needn't show every extreme that they name: `schur_block`: each block is symmetric positive definite. `coarse_inverse`: each cluster's matrix is symmetric positive definite.
All inputs are finite; a program needn't handle non-finite values. No bound on the sum of `glue_link` on one device may be relied on, other than what follows from the above.
Results may differ from a plain program's by a relative error of at most 0.0007.
Values sent between devices are 32-bit elements; how exact they have to be, the bound alone decides.
A program may use at most 64 MiB of HBM per device.

v0:
```python
import jax
import jax.numpy as jnp
from jax import lax
from jax.sharding import PartitionSpec as P

NC = 64
NI = 128
ITERS = 3


highest = lax.Precision.HIGHEST


def shifted(block, axis, distance):
    devices = range(lax.axis_size(axis))
    route = [((i - distance) % len(devices), i) for i in devices]
    return lax.ppermute(block, axis, route)


def inner(first_vec, second_vec):
    return jnp.sum(first_vec * second_vec, axis=0)


def per_device(
    schur_block,
    load_cases,
    precond_scale,
    coarse_basis,
    coarse_inverse,
    corner_weight,
    corner_index,
    iface_block,
    glue_link,
):
    matrix = schur_block[0, 0]
    loads_here = load_cases[0, 0]
    weights = precond_scale[0, 0][:, None]
    basis_rows = coarse_basis[0, 0]
    inverse_rows = coarse_inverse[0]
    owner_gains = corner_weight[0]
    corners = corner_index[0, 0]
    blocks = iface_block[0, 0]
    glue_flag = glue_link[0].astype(jnp.float32)
    owned_count = owner_gains.shape[0]
    corner_total = owned_count * lax.axis_size("sub")
    selector = (corners[:, None] == jnp.arange(corner_total, dtype=jnp.int32)[None, :]).astype(
        jnp.float32
    )
    left_row = NC + blocks[0] * NI
    right_row = NC + blocks[1] * NI

    def precondition(vector):
        pieces = jnp.dot(basis_rows, vector, precision=highest, preferred_element_type=jnp.float32)
        gathered = lax.all_gather(pieces, "sub", axis=0, tiled=True)
        coarse = jnp.dot(
            inverse_rows, gathered, precision=highest, preferred_element_type=jnp.float32
        )
        return weights * vector + jnp.einsum(
            "nw,nr->wr", basis_rows, coarse, precision=highest, preferred_element_type=jnp.float32
        )

    solution = jnp.zeros_like(loads_here)
    residual = loads_here
    precond = precondition(residual)
    direction = precond
    rho_now = lax.psum(inner(residual, precond), ("cluster", "sub"))
    for iteration in range(ITERS):
        applied = jnp.dot(
            matrix, direction.astype(jnp.bfloat16), preferred_element_type=jnp.float32
        )
        corner_rows = direction[:NC]
        owned = lax.psum_scatter(
            jnp.einsum(
                "jk,jr->kr",
                selector,
                corner_rows,
                precision=highest,
                preferred_element_type=jnp.float32,
            ),
            "sub",
            scatter_dimension=0,
            tiled=True,
        )
        scaled = owned * owner_gains[:, None]
        back = jnp.einsum(
            "jk,kr->jr",
            selector,
            lax.all_gather(scaled, "sub", axis=0, tiled=True),
            precision=highest,
            preferred_element_type=jnp.float32,
        )
        applied = jnp.concatenate([applied[:NC] + back, applied[NC:]], axis=0)
        left_block = lax.dynamic_slice_in_dim(direction, left_row, NI, 0)
        right_block = lax.dynamic_slice_in_dim(direction, right_row, NI, 0)
        prev_right, prev_glue = shifted((right_block, glue_flag), "cluster", 1)
        next_left = shifted(left_block, "cluster", -1)
        jump_right = glue_flag[0] * (right_block - next_left)
        jump_left = prev_glue[0] * (prev_right - left_block)
        applied = lax.dynamic_update_slice_in_dim(
            applied, lax.dynamic_slice_in_dim(applied, right_row, NI, 0) + jump_right, right_row, 0
        )
        applied = lax.dynamic_update_slice_in_dim(
            applied, lax.dynamic_slice_in_dim(applied, left_row, NI, 0) - jump_left, left_row, 0
        )
        curve = lax.psum(inner(direction, applied), ("cluster", "sub"))
        step_size = rho_now / curve
        solution = solution + step_size * direction
        if iteration + 1 < ITERS:
            residual = residual - step_size * applied
            precond = precondition(residual)
            rho_next = lax.psum(inner(residual, precond), ("cluster", "sub"))
            direction = precond + rho_next / rho_now * direction
            rho_now = rho_next
    return solution[None, None]


def solution(mesh):
    in_specs = (
        P("cluster", "sub", None, None),
        P("cluster", "sub", None, None),
        P("cluster", "sub", None),
        P("cluster", "sub", None, None),
        P("cluster", "sub", None),
        P("cluster", "sub"),
        P("cluster", "sub", None),
        P("cluster", "sub", None),
        P("cluster", "sub"),
    )
    out_specs = P("cluster", "sub", None, None)
    return jax.shard_map(
        per_device, mesh=mesh, in_specs=in_specs, out_specs=out_specs, check_vma=False
    )
```

profile of v0, /device:TPU:1, one launch (start us, length us, event | category | flops | bytes accessed | tf_op | source)
XLA Modules:
  0.0 1135.0 jit_solution(11785621884392652291)
XLA Ops:
  6.5 1.4 convolution_bitcast_fusion.5
  7.9 44.0 %all-gather = f32[32,6,64]{2,1,0:T(8,128)S(1)} all-gather(f32[1,6,64]{2,1,0:T(8,128)S(1)} %convolution_bitcast_fusion.5), channel_id=1, replica_groups=mesh['cluster'=16,'sub'=32] {'sub'}, dimensions={0}, use_global_device_ids=true | all-gather | bytes 50688 | tf_op jit(solution)/shard_map/all_gather | solution.py:54
  51.9 0.9 fusion.61
  52.8 1.4 fusion.17
  54.2 1.8 fusion.28
  56.1 1.4 fusion.66
  58.2 10.7 collective-permute-start
  69.5 2.6 collective-permute-start.1
  72.8 0.8 fusion.6
  73.7 99.0 %reduce-scatter.4.cloned.1.call-done = f32[16,64]{1,0:T(8,128)} async-done(((f32[512,64]{1,0:T(8,128)}), f32[16,64]{1,0:T(8,128)}) %reduce-scatter.4.cloned.1.call-update) | async-done | bytes 4112 | tf_op jit(solution)/shard_map/reduce_scatter | solution.py:72
  172.7 0.8 broadcast_multiply_fusion.2
  173.5 45.6 %all_gather.19 = f32[512,64]{1,0:T(8,128)S(1)} all-gather(f32[16,64]{1,0:T(8,128)S(1)} %broadcast_multiply_fusion.2), channel_id=1, replica_groups=mesh['cluster'=16,'sub'=32] {'sub'}, dimensions={0}, use_global_device_ids=true | all-gather | bytes 135168 | tf_op jit(solution)/shard_map/all_gather | solution.py:88
  219.1 0.4 convolution_add_fusion.2
  219.7 2.2 collective-permute-start.2
  221.9 0.1 pad_maximum_fusion
  222.0 0.6 dynamic_update_slice.18
  222.6 4.0 collective-permute-done.2
  226.6 0.7 multiply_subtract_fusion.3
  227.3 0.6 dynamic_update_slice.19
  227.9 0.1 multiply_reduce_fusion.4
  228.0 95.8 %all-reduce = (f32[64]{0:T(128)S(1)}, f32[64]{0:T(128)S(1)}) all-reduce(f32[64]{0:T(128)S(1)} %get-tuple-element.6, f32[64]{0:T(128)S(1)} %get-tuple-element.5), channel_id=1, replica_groups=mesh['cluster'=16,'sub'=32] {'cluster','sub'}, use_global_device_ids=true, to_apply=%region_1.0 | all-reduce | flops 128 | bytes 1024 | tf_op jit(solution)/shard_map/psum | solution.py:66
  324.0 0.3 convolution_bitcast_fusion.4
  324.3 39.2 %all-gather.1 = f32[32,6,64]{2,1,0:T(8,128)S(1)} all-gather(f32[1,6,64]{2,1,0:T(8,128)S(1)} %convolution_bitcast_fusion.4), channel_id=1, replica_groups=mesh['cluster'=16,'sub'=32] {'sub'}, dimensions={0}, use_global_device_ids=true | all-gather | bytes 50688 | tf_op jit(solution)/shard_map/all_gather | solution.py:54
  363.5 0.2 fusion.59
  363.6 0.6 multiply_reduce_fusion.3
  364.2 95.5 %psum.44 = f32[64]{0:T(128)S(1)} all-reduce(f32[64]{0:T(128)S(1)} %get-tuple-element.17), channel_id=1, replica_groups=mesh['cluster'=16,'sub'=32] {'cluster','sub'}, use_global_device_ids=true, to_apply=%region_6.0 | all-reduce | flops 64 | bytes 512 | tf_op jit(solution)/shard_map/psum | solution.py:111
  459.8 1.1 fusion.26
  461.0 0.8 fusion.9
  461.8 0.1 slice.51
  462.0 3.5 collective-permute-start.3
  465.5 108.9 %reduce-scatter.6.cloned.1.call-done = f32[16,64]{1,0:T(8,128)} async-done(((f32[512,64]{1,0:T(8,128)}), f32[16,64]{1,0:T(8,128)}) %reduce-scatter.6.cloned.1.call-update) | async-done | bytes 4112 | tf_op jit(solution)/shard_map/reduce_scatter | solution.py:72
  574.4 0.8 broadcast_multiply_fusion.1
  575.2 45.4 %all_gather.21 = f32[512,64]{1,0:T(8,128)S(1)} all-gather(f32[16,64]{1,0:T(8,128)S(1)} %broadcast_multiply_fusion.1), channel_id=1, replica_groups=mesh['cluster'=16,'sub'=32] {'sub'}, dimensions={0}, use_global_device_ids=true | all-gather | bytes 135168 | tf_op jit(solution)/shard_map/all_gather | solution.py:88
  620.5 0.4 convolution_add_fusion.1
  620.9 0.7 constant_dynamic-slice_fusion.3
  621.6 2.3 collective-permute-start.4
  623.9 0.1 pad_maximum_fusion.1
  624.1 0.6 dynamic_update_slice.20
  624.7 4.2 collective-permute-done.4
  628.8 0.7 multiply_subtract_fusion.2
  629.6 0.6 dynamic_update_slice.21
  630.2 0.1 multiply_reduce_fusion.2
  630.3 95.8 %psum.45 = f32[64]{0:T(128)S(1)} all-reduce(f32[64]{0:T(128)S(1)} %multiply_reduce_fusion.2), channel_id=1, replica_groups=mesh['cluster'=16,'sub'=32] {'cluster','sub'}, use_global_device_ids=true, to_apply=%region_9.0 | all-reduce | flops 64 | bytes 512 | tf_op jit(solution)/shard_map/psum | solution.py:105
  726.2 0.3 convolution_bitcast_fusion.3
  726.5 39.1 %all-gather.2 = f32[32,6,64]{2,1,0:T(8,128)S(1)} all-gather(f32[1,6,64]{2,1,0:T(8,128)S(1)} %convolution_bitcast_fusion.3), channel_id=1, replica_groups=mesh['cluster'=16,'sub'=32] {'sub'}, dimensions={0}, use_global_device_ids=true | all-gather | bytes 50688 | tf_op jit(solution)/shard_map/all_gather | solution.py:54
  765.6 0.2 fusion.57
  765.8 0.6 multiply_reduce_fusion.1
  766.3 95.8 %psum.46 = f32[64]{0:T(128)S(1)} all-reduce(f32[64]{0:T(128)S(1)} %get-tuple-element.19), channel_id=1, replica_groups=mesh['cluster'=16,'sub'=32] {'cluster','sub'}, use_global_device_ids=true, to_apply=%region_11.0 | all-reduce | flops 64 | bytes 512 | tf_op jit(solution)/shard_map/psum | solution.py:111
  862.2 1.1 fusion.24
  863.3 0.8 fusion.12
  864.1 0.1 slice.54
  864.3 3.4 collective-permute-start.5
  867.7 108.9 %reduce-scatter.8.cloned.1.call-done = f32[16,64]{1,0:T(8,128)} async-done(((f32[512,64]{1,0:T(8,128)}), f32[16,64]{1,0:T(8,128)}) %reduce-scatter.8.cloned.1.call-update) | async-done | bytes 4112 | tf_op jit(solution)/shard_map/reduce_scatter | solution.py:72
  976.7 0.8 broadcast_multiply_fusion
  977.4 45.4 %all_gather.23 = f32[512,64]{1,0:T(8,128)S(1)} all-gather(f32[16,64]{1,0:T(8,128)S(1)} %broadcast_multiply_fusion), channel_id=1, replica_groups=mesh['cluster'=16,'sub'=32] {'sub'}, dimensions={0}, use_global_device_ids=true | all-gather | bytes 135168 | tf_op jit(solution)/shard_map/all_gather | solution.py:88
  1022.8 0.4 convolution_add_fusion
  1023.3 2.3 collective-permute-start.6
  1025.6 0.1 pad_maximum_fusion.2
  1025.8 0.6 dynamic_update_slice.22
  1026.4 3.9 collective-permute-done.6
  1030.3 0.7 multiply_subtract_fusion.1
  1031.0 0.6 dynamic_update_slice.23
  1031.8 95.8 %psum.47 = f32[64]{0:T(128)S(1)} all-reduce(f32[64]{0:T(128)S(1)} %multiply_reduce_fusion), channel_id=1, replica_groups=mesh['cluster'=16,'sub'=32] {'cluster','sub'}, use_global_device_ids=true, to_apply=%region_14.0 | all-reduce | flops 64 | bytes 512 | tf_op jit(solution)/shard_map/psum | solution.py:105
  1127.6 0.8 add_bitcast_fusion
  (43 shorter events, 1.3 us)
Async XLA Ops:
  6.5 66.2 %copy-start = (bf16[1,1,1024,1024]{3,2,1,0:T(8,128)(2,1)S(1)}, bf16[1,1,1024,1024]{3,2,1,0:T(8,128)(2,1)}, u32[]{:S(2)}) copy-start(bf16[1,1,1024,1024]{3,2,1,0:T(8,128)(2,1)} %param.9) | copy-start | bytes 6291460
  6.5 166.2 %reduce-scatter.4.cloned.1.call-start = ((), (), s32[]{:S(2)}) async-start(), calls=%async_computation.3 | async-start | bytes 270336 | tf_op jit(solution)/shard_map/reduce_scatter | solution.py:72
  52.8 119.9 %copy-start.6 = (f32[1,16]{1,0:T(1,128)S(1)}, f32[1,16]{1,0:T(1,128)}, u32[]{:S(2)}) copy-start(f32[1,16]{1,0:T(1,128)} %param.14) | copy-start | bytes 196
  54.2 164.9 %copy-start.5 = (s32[1,1,64]{2,1,0:T(1,128)S(1)}, s32[1,1,64]{2,1,0:T(1,128)}, u32[]{:S(2)}) copy-start(s32[1,1,64]{2,1,0:T(1,128)} %param.15) | copy-start | bytes 772
  56.1 518.3 %reduce-scatter.6.cloned.1.call-start = ((), (), s32[]{:S(2)}) async-start(), calls=%async_computation.4 | async-start | bytes 270336 | tf_op jit(solution)/shard_map/reduce_scatter | solution.py:72
  58.2 161.4 %collective-permute-start = (f32[128,64]{0,1:T(8,128)S(1)}, f32[128,64]{0,1:T(8,128)S(1)}, u32[]{:S(2)}, u32[]{:S(2)}) collective-permute-start(f32[128,64]{0,1:T(8,128)S(1)} %constant_dynamic-slice_fusion.4), channel_id=1, source_target_pairs={{32,0},{64,32},{96,64},{128,96},{160,128},{192,160},{224,192},{256... | collective-permute-start | bytes 98312 | tf_op jit(solution)/shard_map/ppermute | solution.py:17
  69.5 153.1 %collective-permute-start.1 = (f32[1]{0:T(128)}, f32[1]{0:T(128)}, u32[]{:S(2)}, u32[]{:S(2)}) collective-permute-start(f32[1]{0:T(128)} %bitcast.13), channel_id=1, source_target_pairs={{480,0},{0,32},{32,64},{64,96},{96,128},{128,160},{160,192},{192,2... | collective-permute-start | bytes 20 | tf_op jit(solution)/shard_map/ppermute | solution.py:17
  72.8 155.1 %copy-start.1 = (f32[1,1,1024,64]{2,3,1,0:T(8,128)S(1)}, f32[1,1,1024,64]{2,3,1,0:T(8,128)}, u32[]{:S(2)}) copy-start(f32[1,1,1024,64]{2,3,1,0:T(8,128)} %param.10) | copy-start | bytes 786436
  73.5 250.4 %copy-start.2 = (f32[1,1,6,1024]{3,1,2,0:T(1,128)S(1)}, f32[1,1,6,1024]{3,1,2,0:T(1,128)}, u32[]{:S(2)}) copy-start(f32[1,1,6,1024]{3,1,2,0:T(1,128)} %param.12) | copy-start | bytes 73732
  73.7 289.8 %copy-start.3 = (f32[1,6,192]{2,0,1:T(1,128)S(1)}, f32[1,6,192]{2,0,1:T(1,128)}, u32[]{:S(2)}) copy-start(f32[1,6,192]{2,0,1:T(1,128)} %param.13) | copy-start | bytes 13828
  173.5 190.2 %copy-start.4 = (f32[1,1,1024]{2,1,0:T(1,128)S(1)}, f32[1,1,1024]{2,1,0:T(1,128)}, u32[]{:S(2)}) copy-start(f32[1,1,1024]{2,1,0:T(1,128)} %param.11) | copy-start | bytes 12292
  219.7 6.9 collective-permute-start.2
  460.9 515.7 %reduce-scatter.8.cloned.1.call-start = ((), (), s32[]{:S(2)}) async-start(), calls=%async_computation.5 | async-start | bytes 270336 | tf_op jit(solution)/shard_map/reduce_scatter | solution.py:72
  462.0 159.0 %collective-permute-start.3 = (f32[128,64]{0,1:T(8,128)S(1)}, f32[128,64]{0,1:T(8,128)S(1)}, u32[]{:S(2)}, u32[]{:S(2)}) collective-permute-start(f32[128,64]{0,1:T(8,128)S(1)} %constant_dynamic-slice_fusion.2), channel_id=1, source_target_pairs={{32,0},{64,32},{96,64},{128,96},{160,128},{192,160},{224,192},{256... | collective-permute-start | bytes 98312 | tf_op jit(solution)/shard_map/ppermute | solution.py:17
  621.6 7.2 collective-permute-start.4
  864.3 158.9 %collective-permute-start.5 = (f32[128,64]{0,1:T(8,128)S(1)}, f32[128,64]{0,1:T(8,128)S(1)}, u32[]{:S(2)}, u32[]{:S(2)}) collective-permute-start(f32[128,64]{0,1:T(8,128)S(1)} %constant_dynamic-slice_fusion), channel_id=1, source_target_pairs={{32,0},{64,32},{96,64},{128,96},{160,128},{192,160},{224,192},{256... | collective-permute-start | bytes 98312 | tf_op jit(solution)/shard_map/ppermute | solution.py:17
  1023.3 7.0 collective-permute-start.6
Sparse Core Ops, SparseCore 0:
  56.2 116.4 reduce-scatter.3
  461.1 113.2 reduce-scatter.5
  863.5 113.1 reduce-scatter.7
where the time goes:
time: 1140 us; the launch traced here: 1130 us
  blocking collectives  737 us (65%)
  waiting for transfers between devices  329 us (29%)
  starting transfers between devices  27.1 us (2%)
  between operations  15.3 us (1%)
  matrix products  13.1 us (1%)
    reduce_scatter x3, waiting for transfers between devices, per_device(): lax.psum_scatter(jnp.einsum('jk,jr->kr', selector, corner_rows, precision...  317 us
    psum x2, blocking collectives, per_device(): curve = lax.psum(inner(direction, applied), ('cluster', 'sub'))  192 us
    psum x2, blocking collectives, per_device(): rho_next = lax.psum(inner(residual, precond), ('cluster', 'sub'))  191 us
    all_gather x3, blocking collectives, per_device(): lax.all_gather(scaled, 'sub', axis=0, tiled=True)  136 us
    all_gather x3, blocking collectives, precondition(): gathered = lax.all_gather(pieces, 'sub', axis=0, tiled=True)  122 us
    psum x1, blocking collectives, per_device(): rho_now = lax.psum(inner(residual, precond), ('cluster', 'sub'))  95.8 us
    ppermute x7, starting transfers between devices, shifted(): return lax.ppermute(block, axis, route)  27 us
  transfers between devices with their start and end apart: 10, of which 6 were waited for; matrix products, arithmetic and copies ran while one was open for 1% of the time, Pallas kernels for 0%

commit v1 on v0

v1 whole, which is shorter than its diff:
```python
import functools

import jax
import jax.numpy as jnp
from jax import lax
from jax.experimental import pallas as pl
from jax.experimental.pallas import tpu as pltpu
from jax.sharding import PartitionSpec as P

NC = 64
NI = 128
ITERS = 3
f32 = jnp.float32
bf16 = jnp.bfloat16


def dot(a, b, dims=((1,), (0,))):
    return lax.dot_general(
        a, b, (dims, ((), ())), precision=lax.Precision.HIGHEST, preferred_element_type=f32
    )


def iota(shape, dim):
    return lax.broadcasted_iota(jnp.int32, shape, dim)


def kernel(
    n_sub, n_cl,
    s_hbm, loads_ref, scale_ref, basis_ref, inv_ref, weight_ref, corner_ref, iface_ref, glue_ref,
    out_ref,
    smat, b8, bt, dmat, zv, dv, xv, sv, qv,
    ohT, oh, ct, invx, inv_own, e_scr, ccol, wcol,
    st_src, st_buf,
    p1_src, p1_buf, rs_src, rs_buf, ag_src, ag_buf, p2_src, p2_buf, gl_src, gl_buf,
    tq, td, tz,
    load_sem, st_sem, p1_sem, rs_sem, ag_sem, p2_sem, gl_sem,
):
    me = lax.axis_index("sub")
    cl = lax.axis_index("cluster")
    n_rows = loads_ref.shape[0]
    r_cols = loads_ref.shape[1]
    nz, cm = basis_ref.shape[0], inv_ref.shape[1]
    own = weight_ref.shape[1]
    half = own // 2
    nb = (n_rows - NC) // NI
    wst = st_src.shape[1]
    blk = 8 * n_sub

    load = pltpu.make_async_copy(s_hbm, smat, load_sem)
    load.start()

    barrier = pltpu.get_barrier_semaphore()

    @pl.loop(1, n_sub)
    def _(step):
        pl.semaphore_signal(barrier, inc=1, device_id={"sub": lax.rem(me + step, n_sub)})

    @pl.loop(1, n_cl)
    def _(step):
        pl.semaphore_signal(barrier, inc=1, device_id={"cluster": lax.rem(cl + step, n_cl)})

    def spread(src_of, buf, sem, axis, here, n):
        @pl.loop(1, n)
        def _(step):
            peer = lax.rem(here + step, n)
            pltpu.make_async_remote_copy(
                src_ref=src_of(peer),
                dst_ref=buf.at[here],
                send_sem=sem.at[0],
                recv_sem=sem.at[1],
                device_id={axis: peer},
            ).start()

    def drain(buf, sem, which, n):
        view = buf.at[pl.ds(0, n - 1)]
        pltpu.make_async_copy(view, view, sem.at[which]).wait()

    b8[0:nz, :] = basis_ref[...]
    b8[nz:nz + 1, :] = scale_ref[...]
    b8[nz + 1:8, :] = jnp.zeros((7 - nz, n_rows), f32)
    bt[...] = jnp.transpose(b8[...])
    pick = ((iota((8, r_cols), 0) == nz)).astype(f32)
    dmat[...] = dot(bt[...], pick)
    b8[nz:nz + 1, :] = jnp.zeros((1, n_rows), f32)

    corner_row = corner_ref[...]
    eye = iota((NC, NC), 0) == iota((NC, NC), 1)
    ccol[...] = jnp.sum(jnp.where(eye, corner_row, 0), axis=1, keepdims=True)

    m = iota((blk, NC), 0)
    base = (m >> 3) * own + (m & 7)
    oh[:, 0:NC] = (base == corner_row).astype(f32)
    oh[:, NC:2 * NC] = (base + half == corner_row).astype(f32)
    m = iota((NC, blk), 1)
    base = (m >> 3) * own + (m & 7)
    ohT[0:NC, :] = (base == ccol[...]).astype(f32)
    ohT[NC:2 * NC, :] = (base + half == ccol[...]).astype(f32)

    st_src[...] = jnp.zeros(st_src.shape, f32)
    st_src[0:nz, 0:cm] = inv_ref[...]
    st_src[0:nz, wst - NC:wst] = basis_ref[:, 0:NC]
    st_src[nz:nz + 1, wst - NC:wst] = corner_row.astype(f32)
    st_src[nz + 1:nz + 2, wst - NC:wst - NC + own] = weight_ref[...]

    ea, eb = iota((wst, blk), 0), iota((wst, blk), 1)
    expand = ((ea == (eb >> 3) * nz + (eb & 7)) & ((eb & 7) < nz) & (ea < cm)).astype(f32)
    row_ok = iota((8, wst), 0) < nz
    inv_own[...] = dot(jnp.where(row_ok, st_src[...], 0.0), expand)

    def packed_corners(v):
        z = jnp.zeros((NC, r_cols), f32)
        vv = jnp.concatenate(
            [jnp.concatenate([v, z], axis=1), jnp.concatenate([z, v], axis=1)], axis=0
        )
        return dot(oh[...], vv)

    def first_message(k, vec, sums):
        pieces = dot(b8[...], vec)
        zero = jnp.zeros((8 - len(sums), r_cols), f32)
        msg = jnp.concatenate([pieces, jnp.concatenate(list(sums) + [zero], axis=0)], axis=1)
        p1_src[k] = msg
        p1_buf[k, me] = msg

    def send_first(k):
        spread(lambda peer: p1_src.at[k], p1_buf.at[k], p1_sem.at[k], "sub", me, n_sub)

    def corner_message(k, vec):
        rs_src[k] = packed_corners(vec).reshape(n_sub, 8, 2 * r_cols)
        rs_buf[k, me] = rs_src[k, me]

    def send_corners(k):
        spread(lambda peer: rs_src.at[k, peer], rs_buf.at[k], rs_sem.at[k], "sub", me, n_sub)

    def own_corners(k):
        drain(rs_buf.at[k], rs_sem.at[k], 1, n_sub)
        total = jnp.sum(rs_buf[k], axis=0)
        ag_src[k] = total
        ag_buf[k, me] = total
        spread(lambda peer: ag_src.at[k], ag_buf.at[k], ag_sem.at[k], "sub", me, n_sub)

    def corner_back(k):
        drain(ag_buf.at[k], ag_sem.at[k], 1, n_sub)
        got = ag_buf[k].reshape(blk, 2 * r_cols)
        quad = dot(ohT[...], got)
        return quad[0:NC, 0:r_cols] + quad[NC:2 * NC, r_cols:2 * r_cols]

    glue_here = glue_ref[...].astype(f32)
    hi = NI // 2

    def placed(side, b):
        return (iface_ref[0:1, 1 - side:2 - side] == b).astype(f32)

    def block_of(side):
        rows = jnp.zeros((NI, r_cols), f32)
        for b in range(nb):
            rows = rows + placed(side, b) * dv[NC + b * NI:NC + (b + 1) * NI, :]
        return rows

    def send_glue(k):
        for side in range(2):
            rows = block_of(side)
            gl_src[k, side, 0:hi, :] = jnp.concatenate([rows[0:hi], rows[hi:NI]], axis=1)
            gl_src[k, side, hi:hi + 8, :] = jnp.broadcast_to(glue_here, (8, 2 * r_cols))
        for side, peer in ((0, lax.rem(cl + 1, n_cl)), (1, lax.rem(cl + n_cl - 1, n_cl))):
            pltpu.make_async_remote_copy(
                src_ref=gl_src.at[k, side],
                dst_ref=gl_buf.at[k, side],
                send_sem=gl_sem.at[k, side, 0],
                recv_sem=gl_sem.at[k, side, 1],
                device_id={"cluster": peer},
            ).start()

    def glue_wait(k, which):
        for side in range(2):
            pltpu.make_async_copy(
                gl_src.at[k, side], gl_buf.at[k, side], gl_sem.at[k, side, which]
            ).wait()

    def unpack(k, side):
        a = gl_buf[k, side, 0:hi, :]
        return jnp.concatenate([a[:, 0:r_cols], a[:, r_cols:2 * r_cols]], axis=0)

    loads = loads_ref[...]
    scaled = dmat[...] * loads
    first_message(0, loads, [jnp.sum(scaled * loads, axis=0, keepdims=True)])
    corner_message(0, scaled[0:NC, :])
    st_buf[me] = st_src[...]

    pl.semaphore_wait(barrier, n_sub + n_cl - 2)

    send_first(0)
    send_corners(0)
    spread(lambda peer: st_src, st_buf, st_sem, "sub", me, n_sub)

    drain(p1_buf.at[0], p1_sem.at[0], 1, n_sub)
    got = p1_buf[0].reshape(blk, 2 * r_cols)
    e_own = dot(inv_own[...], got)[:, 0:r_cols]
    zv[...] = dmat[...] * loads + dot(bt[...], e_own * (iota((8, r_cols), 0) < nz).astype(f32))
    dv[...] = zv[...]
    send_glue(0)
    own_corners(0)
    load.wait()

    def product():
        sv[...] = jnp.dot(smat[...], dv[...].astype(bf16), preferred_element_type=f32)

    product()

    drain(st_buf, st_sem, 1, n_sub)
    ws = jnp.zeros((NC, 1), f32)
    lane = iota((NC, NC), 1)
    row8 = iota((8, NC), 0) < nz
    for s in range(n_sub):
        tile = st_buf[s, :, wst - NC:wst]
        match = (ccol[...].astype(f32) == tile[nz:nz + 1, :]).astype(f32)
        ct[8 * s:8 * s + 8, :] = dot(jnp.where(row8, tile, 0.0), match, ((1,), (1,)))
        mine = (ccol[...] == s * own + lane) & (lane < own)
        ws = ws + jnp.sum(jnp.where(mine, tile[nz + 1:nz + 2, :], 0.0), axis=1, keepdims=True)
    wcol[...] = ws
    rows_ok = ((iota((blk, wst), 0) & 7) < nz) & (iota((blk, wst), 1) < cm)
    invx[...] = dot(jnp.where(rows_ok, st_buf[...].reshape(blk, wst), 0.0), expand)

    def coarse(k):
        got = p1_buf[k].reshape(blk, 2 * r_cols)
        e_all = dot(invx[...], got)
        e_scr[...] = e_all[:, 0:r_cols]
        quad = jnp.sum((got * e_all)[:, 0:r_cols], axis=0, keepdims=True)
        return quad, jnp.sum(p1_buf[k], axis=0)[:, r_cols:2 * r_cols]

    quad, sums = coarse(0)
    rho_part = sums[0:1, :] + quad
    tz[...] = corner_back(0) + dot(ct[...], e_scr[...], ((0,), (0,)))
    td[...] = tz[...]
    xv[...] = jnp.zeros_like(xv)

    def finish_product(k):
        sv[0:NC, :] = sv[0:NC, :] + wcol[...] * td[...]
        glue_wait(k, 1)
        next_left = unpack(k, 1)
        prev_right = unpack(k, 0)
        prev_glue = gl_buf[k, 0, hi:hi + 1, 0:r_cols]
        jump_right = glue_here * (block_of(0) - next_left)
        jump_left = prev_glue * (prev_right - block_of(1))
        for b in range(nb):
            rows = slice(NC + b * NI, NC + (b + 1) * NI)
            sv[rows, :] = sv[rows, :] + placed(0, b) * jump_right - placed(1, b) * jump_left

    rho = None
    for k in range(ITERS):
        last = k + 1 == ITERS
        finish_product(k)
        s, d = sv[...], dv[...]
        sums = [jnp.sum(d * s, axis=0, keepdims=True)]
        if not last:
            ds = dmat[...] * s
            sums.append(jnp.sum(zv[...] * s, axis=0, keepdims=True))
            sums.append(jnp.sum(ds * s, axis=0, keepdims=True))
            first_message(k + 1, s, sums)
            send_first(k + 1)
            corner_message(k + 1, ds[0:NC, :])
            send_corners(k + 1)
        else:
            first_message(k + 1, s, sums)
            send_first(k + 1)
        drain(p1_buf.at[k + 1], p1_sem.at[k + 1], 1, n_sub)
        if not last:
            quad, sums = coarse(k + 1)
            parts = [sums[0:1], sums[1:2], sums[2:3] + quad]
        else:
            sums = jnp.sum(p1_buf[k + 1], axis=0)[:, r_cols:2 * r_cols]
            parts = [sums[0:1], sums[1:2], sums[2:3]]
        msg = jnp.concatenate(
            [
                jnp.concatenate([parts[0], parts[1]], axis=1),
                jnp.concatenate([parts[2], rho_part], axis=1),
            ],
            axis=0,
        )
        p2_src[k] = msg
        p2_buf[k, cl] = msg
        spread(lambda peer: p2_src.at[k], p2_buf.at[k], p2_sem.at[k], "cluster", cl, n_cl)
        if not last:
            e_own = e_scr[pl.ds(8 * me, 8), :]
            q = ds + dot(bt[...], e_own)
            qv[...] = q
            tq[...] = dot(ct[...], e_scr[...], ((0,), (0,)))
            own_corners(k + 1)
        drain(p2_buf.at[k], p2_sem.at[k], 1, n_cl)
        total = jnp.sum(p2_buf[k], axis=0)
        curve = total[0:1, 0:r_cols]
        if k == 0:
            rho = total[1:2, r_cols:2 * r_cols]
        step = rho / curve
        if last:
            out_ref[...] = xv[...] + step * dv[...]
            break
        xv[...] = xv[...] + step * dv[...]
        zs = total[0:1, r_cols:2 * r_cols]
        sq = total[1:2, 0:r_cols]
        rho_next = rho - 2.0 * step * zs + step * (step * sq)
        beta = rho_next / rho
        z = zv[...] - step * qv[...]
        zv[...] = z
        dv[...] = z + beta * dv[...]
        rho = rho_next
        send_glue(k + 1)
        product()
        tz[...] = tz[...] - step * (tq[...] + corner_back(k + 1))
        td[...] = tz[...] + beta * td[...]

    drain(st_buf, st_sem, 0, n_sub)
    for k in range(ITERS + 1):
        drain(p1_buf.at[k], p1_sem.at[k], 0, n_sub)
    for k in range(ITERS):
        drain(rs_buf.at[k], rs_sem.at[k], 0, n_sub)
        drain(ag_buf.at[k], ag_sem.at[k], 0, n_sub)
        drain(p2_buf.at[k], p2_sem.at[k], 0, n_cl)
        glue_wait(k, 0)


def per_device(
    n_sub, n_cl, schur_block, load_cases, precond_scale, coarse_basis, coarse_inverse,
    corner_weight, corner_index, iface_block, glue_link,
):
    n_rows, r = load_cases.shape[2:]
    nz, cm = coarse_basis.shape[2], coarse_inverse.shape[2]
    blk = 8 * n_sub
    wst = -(-(cm + NC) // 128) * 128
    vec = pltpu.VMEM((n_rows, r), f32)
    vmem = pl.BlockSpec(memory_space=pltpu.VMEM)
    dma = pltpu.SemaphoreType.DMA
    out = pl.pallas_call(
        functools.partial(kernel, n_sub, n_cl),
        out_shape=jax.ShapeDtypeStruct((n_rows, r), f32),
        in_specs=[pl.BlockSpec(memory_space=pl.ANY)] + [vmem] * 8,
        out_specs=vmem,
        scratch_shapes=[
            pltpu.VMEM((n_rows, n_rows), bf16),
            pltpu.VMEM((8, n_rows), f32),
            pltpu.VMEM((n_rows, 8), f32),
            vec, vec, vec, vec, vec, vec,
            pltpu.VMEM((2 * NC, blk), f32),
            pltpu.VMEM((blk, 2 * NC), f32),
            pltpu.VMEM((blk, NC), f32),
            pltpu.VMEM((blk, blk), f32),
            pltpu.VMEM((8, blk), f32),
            pltpu.VMEM((blk, r), f32),
            pltpu.VMEM((NC, 1), jnp.int32),
            pltpu.VMEM((NC, 1), f32),
            pltpu.VMEM((8, wst), f32),
            pltpu.VMEM((n_sub, 8, wst), f32),
            pltpu.VMEM((ITERS + 1, 8, 2 * r), f32),
            pltpu.VMEM((ITERS + 1, n_sub, 8, 2 * r), f32),
            pltpu.VMEM((ITERS, n_sub, 8, 2 * r), f32),
            pltpu.VMEM((ITERS, n_sub, 8, 2 * r), f32),
            pltpu.VMEM((ITERS, 8, 2 * r), f32),
            pltpu.VMEM((ITERS, n_sub, 8, 2 * r), f32),
            pltpu.VMEM((ITERS, 2, 2 * r), f32),
            pltpu.VMEM((ITERS, n_cl, 2, 2 * r), f32),
            pltpu.VMEM((ITERS, 2, NI // 2 + 8, 2 * r), f32),
            pltpu.VMEM((ITERS, 2, NI // 2 + 8, 2 * r), f32),
            pltpu.VMEM((NC, r), f32),
            pltpu.VMEM((NC, r), f32),
            pltpu.VMEM((NC, r), f32),
            dma(()),
            dma((2,)),
            dma((ITERS + 1, 2)),
            dma((ITERS, 2)),
            dma((ITERS, 2)),
            dma((ITERS, 2)),
            dma((ITERS, 2, 2)),
        ],
        compiler_params=pltpu.CompilerParams(
            collective_id=0, has_side_effects=True, vmem_limit_bytes=48 * 1024 * 1024
        ),
    )(
        schur_block[0, 0], load_cases[0, 0], precond_scale[0], coarse_basis[0, 0],
        coarse_inverse[0], corner_weight, corner_index[0], iface_block[0], glue_link,
    )
    return out[None, None]


def solution(mesh):
    in_specs = (
        P("cluster", "sub", None, None),
        P("cluster", "sub", None, None),
        P("cluster", "sub", None),
        P("cluster", "sub", None, None),
        P("cluster", "sub", None),
        P("cluster", "sub"),
        P("cluster", "sub", None),
        P("cluster", "sub", None),
        P("cluster", "sub"),
    )
    return jax.shard_map(
        functools.partial(per_device, mesh.shape["sub"], mesh.shape["cluster"]),
        mesh=mesh, in_specs=in_specs, out_specs=P("cluster", "sub", None, None), check_vma=False,
    )
```

time: 1140 us -> 97.8 us (0.09)
  blocking collectives: 737 us -> 0 us
  waiting for transfers between devices: 329 us -> 0 us
  Pallas kernels: 0 us -> 89.1 us
  starting transfers between devices: 27.1 us -> 0 us
  between operations: 15.3 us -> 0.68 us
  matrix products: 13.1 us -> 0 us
    psum x5 -> x0, blocking collectives: 479 us -> none  [the longest x2 192 us: per_device(): curve = lax.psum(inner(direction, applied), ('cluster', 'sub'))]
    reduce_scatter x3 -> x0, waiting for transfers between devices: 317 us -> none  [per_device(): lax.psum_scatter(jnp.einsum('jk,jr->kr', selector, corner_rows, precision...]
    all_gather x6 -> x0, blocking collectives: 259 us -> none  [the longest x3 136 us: per_device(): lax.all_gather(scaled, 'sub', axis=0, tiled=True)]
    pallas_call x0 -> x1, Pallas kernels: none -> 89.1 us  [per_device(): pl.pallas_call(functools.partial(kernel, n_sub, n_cl), out_shape=jax.Shap...]
    ppermute x7 -> x0, starting transfers between devices: 27 us -> none  [shifted(): return lax.ppermute(block, axis, route)]
    dot_general x18 -> x0, matrix products: 13.1 us -> none  [the longest x3 4 us: per_device(): jnp.einsum('jk,jr->kr', selector, corner_rows, precision=highest, preferr...]
    ppermute x7 -> x0, waiting for transfers between devices: 12.1 us -> none  [shifted(): return lax.ppermute(block, axis, route)]
  transfers between devices with their start and end apart: 10 -> 0, of which waited for: 6 -> 0; matrix products, arithmetic and copies ran while one was open for 1% -> 0% of each run, Pallas kernels for 0% -> 0%
where the time goes in v1:
time: 97.8 us; the launch traced here: 97.5 us
  Pallas kernels  89.1 us (91%)
  local copies, waits for them, and re-layouts  7.71 us (8%)
    pallas_call x1, Pallas kernels, per_device(): pl.pallas_call(functools.partial(kernel, n_sub, n_cl), out_shape=jax.Shap...  89.1 us
    unnamed x13, local copies, waits for them, and re-layouts  6.82 us

profile of v1, /device:TPU:1, one launch (start us, length us, event | category | flops | bytes accessed | tf_op | source)
XLA Modules:
  0.0 97.5 jit_solution(9518416359997935051)
XLA Ops:
  0.7 0.7 copy.17
  1.3 0.7 copy.16
  2.1 1.1 %copy.10 = f32[1,1,1024,64]{3,2,1,0:T(8,128)S(1)} copy(f32[1,1,1024,64]{2,3,1,0:T(8,128)} %param.10) | data formatting | bytes 524288 | tf_op args[1]
  3.2 0.0 copy-start
  3.3 1.6 %copy-done = bf16[1,1,1024,1024]{3,2,1,0:T(8,128)(2,1)S(1)} copy-done((bf16[1,1,1024,1024]{3,2,1,0:T(8,128)(2,1)S(1)}, bf16[1,1,1024,1024]{3,2,1,0:T(8,128)(2,1)}, u32[]{:S(2)}) %copy-start) | copy-done | bytes 2097176
  4.8 0.0 copy-start.1
  4.8 0.7 copy-done.1
  5.5 0.0 copy-start.2
  5.5 0.7 copy-done.2
  6.2 0.0 copy-start.3
  6.2 0.7 copy-done.3
  6.8 0.0 copy-start.4
  6.8 0.7 copy-done.4
  7.5 89.1 %shard_map.91 = f32[1024,64]{1,0:T(8,128)S(1)} custom-call(bf16[1024,1024]{1,0:T(8,128)(2,1)S(1)} %bitcast.12, f32[1024,64]{1,0:T(8,128)S(1)} %bitcast.14, f32[1,1024]{1,0:T(1,128)S(1)} %bitcast.17, f32[6,1024]{1,0:T(8,128)S(1)} %bitcast.15, f32[6,192]{1,0:T(8,128)S(1)} %bitcast.16, f32[1,16]{1,0:T(1,128)S(1)} %copy-done.2, s32[1,64]{1,0:T(1,128)S(1)} %bitcast.18, ...), custom_call_target="tpu_custom_call" | custom-call | tf_op jit(solution)/shard_map/pallas_call | solution.py:332
  96.6 0.9 copy.11
Async XLA Ops:
  3.2 1.6 %copy-start = (bf16[1,1,1024,1024]{3,2,1,0:T(8,128)(2,1)S(1)}, bf16[1,1,1024,1024]{3,2,1,0:T(8,128)(2,1)}, u32[]{:S(2)}) copy-start(bf16[1,1,1024,1024]{3,2,1,0:T(8,128)(2,1)} %param.9) | copy-start | bytes 6291460
  4.8 0.7 copy-start.1
  5.5 0.7 copy-start.2
  6.2 0.7 copy-start.3
  6.8 0.7 copy-start.4

commit v2 on v1

--- a/solution.py
+++ b/solution.py
@@ -26,9 +26,11 @@
 
 def kernel(
     n_sub, n_cl,
-    s_hbm, loads_ref, scale_ref, basis_ref, inv_ref, weight_ref, corner_ref, iface_ref, glue_ref,
+    s_hbm, loads_hbm, scale_hbm, basis_hbm, inv_hbm, weight_hbm, corner_hbm, iface_hbm, glue_hbm,
     out_ref,
-    smat, b8, bt, dmat, zv, dv, xv, sv, qv,
+    smat, loads_t, scale_ref, basis_ref, inv_ref, weight_ref, corner_ref, iface_ref, glue_ref,
+    lv, nld, prd, nlz, prz, scol,
+    b8, bt, dmat, zv, dv, xv, sv, qv,
     ohT, oh, ct, invx, inv_own, e_scr, ccol, wcol,
     st_src, st_buf,
     p1_src, p1_buf, rs_src, rs_buf, ag_src, ag_buf, p2_src, p2_buf, gl_src, gl_buf,
@@ -37,18 +39,14 @@
 ):
     me = lax.axis_index("sub")
     cl = lax.axis_index("cluster")
-    n_rows = loads_ref.shape[0]
-    r_cols = loads_ref.shape[1]
-    nz, cm = basis_ref.shape[0], inv_ref.shape[1]
+    r_cols, n_rows = loads_t.shape
+    nz, cm = basis_ref.shape[0], inv_ref.shape[2]
     own = weight_ref.shape[1]
     half = own // 2
     nb = (n_rows - NC) // NI
     wst = st_src.shape[1]
     blk = 8 * n_sub
 
-    load = pltpu.make_async_copy(s_hbm, smat, load_sem)
-    load.start()
-
     barrier = pltpu.get_barrier_semaphore()
 
     @pl.loop(1, n_sub)
@@ -59,23 +57,36 @@
     def _(step):
         pl.semaphore_signal(barrier, inc=1, device_id={"cluster": lax.rem(cl + step, n_cl)})
 
-    def spread(src_of, buf, sem, axis, here, n):
-        @pl.loop(1, n)
-        def _(step):
-            peer = lax.rem(here + step, n)
+    fields = (
+        (loads_hbm, loads_t), (basis_hbm, basis_ref), (scale_hbm, scale_ref), (inv_hbm, inv_ref),
+        (corner_hbm, corner_ref), (weight_hbm, weight_ref), (iface_hbm, iface_ref),
+        (glue_hbm, glue_ref), (s_hbm, smat),
+    )
+    copies = [pltpu.make_async_copy(a, b, load_sem.at[i]) for i, (a, b) in enumerate(fields)]
+    for copy in copies:
+        copy.start()
+
+    def spread(src_of, buf, sem, axis, here, n, rows=8):
+        @pl.loop(0, n - 1)
+        def _(i):
+            sign = 1 - 2 * lax.rem(i, 2)
+            peer = lax.rem(here + n // 2 + sign * lax.div(i + 1, 2), n)
             pltpu.make_async_remote_copy(
-                src_ref=src_of(peer),
-                dst_ref=buf.at[here],
+                src_ref=src_of(peer).at[pl.ds(0, rows)],
+                dst_ref=buf.at[here, pl.ds(0, rows)],
                 send_sem=sem.at[0],
                 recv_sem=sem.at[1],
                 device_id={axis: peer},
             ).start()
 
-    def drain(buf, sem, which, n):
-        view = buf.at[pl.ds(0, n - 1)]
+    def drain(buf, sem, which, n, rows=8):
+        view = buf.at[pl.ds(0, n - 1), pl.ds(0, rows)]
         pltpu.make_async_copy(view, view, sem.at[which]).wait()
 
-    b8[0:nz, :] = basis_ref[...]
+    for copy in copies[:-1]:
+        copy.wait()
+    for i in range(nz):
+        b8[i:i + 1, :] = basis_ref[i]
     b8[nz:nz + 1, :] = scale_ref[...]
     b8[nz + 1:8, :] = jnp.zeros((7 - nz, n_rows), f32)
     bt[...] = jnp.transpose(b8[...])
@@ -97,8 +108,10 @@
     ohT[NC:2 * NC, :] = (base + half == ccol[...]).astype(f32)
 
     st_src[...] = jnp.zeros(st_src.shape, f32)
-    st_src[0:nz, 0:cm] = inv_ref[...]
-    st_src[0:nz, wst - NC:wst] = basis_ref[:, 0:NC]
+    for i in range(nz):
+        st_src[i:i + 1, 0:cm] = inv_ref[i]
+    st_src[0:nz, wst - NC:wst] = b8[0:nz, 0:NC]
+    st_src[nz:nz + 1, 0:NC] = scale_ref[:, 0:NC]
     st_src[nz:nz + 1, wst - NC:wst] = corner_row.astype(f32)
     st_src[nz + 1:nz + 2, wst - NC:wst - NC + own] = weight_ref[...]
 
@@ -114,15 +127,32 @@
         )
         return dot(oh[...], vv)
 
+    tail = jnp.zeros((3, r_cols), f32)
+
     def first_message(k, vec, sums):
         pieces = dot(b8[...], vec)
-        zero = jnp.zeros((8 - len(sums), r_cols), f32)
-        msg = jnp.concatenate([pieces, jnp.concatenate(list(sums) + [zero], axis=0)], axis=1)
+        sums = list(sums) + [jnp.zeros((1, r_cols), f32)] * (4 - len(sums))
+        msg = jnp.concatenate(
+            [
+                jnp.concatenate([pieces[0:3], sums[0], sums[1], tail], axis=0),
+                jnp.concatenate([pieces[3:6], sums[2], sums[3], tail], axis=0),
+            ],
+            axis=1,
+        )
         p1_src[k] = msg
         p1_buf[k, me] = msg
 
     def send_first(k):
-        spread(lambda peer: p1_src.at[k], p1_buf.at[k], p1_sem.at[k], "sub", me, n_sub)
+        spread(lambda peer: p1_src.at[k], p1_buf.at[k], p1_sem.at[k], "sub", me, n_sub, 5)
+
+    def first_received(k):
+        drain(p1_buf.at[k], p1_sem.at[k], 1, n_sub, 5)
+        got = p1_buf[k]
+        at = iota(got.shape, 1)
+        got = jnp.where(at < 5, got, 0.0)
+        moved = pltpu.roll(pltpu.roll(got, r_cols, 2), 3, 1)
+        pieces = jnp.where(at < 3, got, jnp.where(at < nz, moved, 0.0))
+        return pieces.reshape(blk, 2 * r_cols)[:, 0:r_cols], jnp.sum(got, axis=0)[3:5]
 
     def corner_message(k, vec):
         rs_src[k] = packed_corners(vec).reshape(n_sub, 8, 2 * r_cols)
@@ -150,15 +180,15 @@
     def placed(side, b):
         return (iface_ref[0:1, 1 - side:2 - side] == b).astype(f32)
 
-    def block_of(side):
+    def block_of(side, ref):
         rows = jnp.zeros((NI, r_cols), f32)
         for b in range(nb):
-            rows = rows + placed(side, b) * dv[NC + b * NI:NC + (b + 1) * NI, :]
+            rows = rows + placed(side, b) * ref[NC + b * NI:NC + (b + 1) * NI, :]
         return rows
 
-    def send_glue(k):
+    def send_glue(k, ref):
         for side in range(2):
-            rows = block_of(side)
+            rows = block_of(side, ref)
             gl_src[k, side, 0:hi, :] = jnp.concatenate([rows[0:hi], rows[hi:NI]], axis=1)
             gl_src[k, side, hi:hi + 8, :] = jnp.broadcast_to(glue_here, (8, 2 * r_cols))
         for side, peer in ((0, lax.rem(cl + 1, n_cl)), (1, lax.rem(cl + n_cl - 1, n_cl))):
@@ -180,95 +210,114 @@
         a = gl_buf[k, side, 0:hi, :]
         return jnp.concatenate([a[:, 0:r_cols], a[:, r_cols:2 * r_cols]], axis=0)
 
-    loads = loads_ref[...]
+    lv[...] = jnp.transpose(loads_t[...])
+    loads = lv[...]
     scaled = dmat[...] * loads
+    corner_message(0, scaled[0:NC, :])
     first_message(0, loads, [jnp.sum(scaled * loads, axis=0, keepdims=True)])
-    corner_message(0, scaled[0:NC, :])
     st_buf[me] = st_src[...]
 
     pl.semaphore_wait(barrier, n_sub + n_cl - 2)
 
+    send_corners(0)
     send_first(0)
-    send_corners(0)
     spread(lambda peer: st_src, st_buf, st_sem, "sub", me, n_sub)
-
-    drain(p1_buf.at[0], p1_sem.at[0], 1, n_sub)
-    got = p1_buf[0].reshape(blk, 2 * r_cols)
-    e_own = dot(inv_own[...], got)[:, 0:r_cols]
-    zv[...] = dmat[...] * loads + dot(bt[...], e_own * (iota((8, r_cols), 0) < nz).astype(f32))
-    dv[...] = zv[...]
-    send_glue(0)
+    copies[-1].wait()
     own_corners(0)
-    load.wait()
-
-    def product():
-        sv[...] = jnp.dot(smat[...], dv[...].astype(bf16), preferred_element_type=f32)
-
-    product()
+    first_pieces, first_sums = first_received(0)
+    e_own = dot(inv_own[...], first_pieces)
+    z = dmat[...] * lv[...] + dot(bt[...], e_own * (iota((8, r_cols), 0) < nz).astype(f32))
+    zv[...] = z
+    dv[...] = z
+
+    def product(k, last):
+        half_d = dv[...].astype(bf16)
+        top = jnp.dot(smat[0:NC, :], half_d, preferred_element_type=f32)
+        sv[0:NC, :] = top
+        if not last:
+            corner_message(k + 1, dmat[0:NC, :] * top)
+            send_corners(k + 1)
+        if k == 0:
+            send_glue(0, zv)
+        sv[NC:, :] = jnp.dot(smat[NC:, :], half_d, preferred_element_type=f32)
+
+    product(0, False)
 
     drain(st_buf, st_sem, 1, n_sub)
     ws = jnp.zeros((NC, 1), f32)
+    sc = jnp.zeros((NC, 1), f32)
     lane = iota((NC, NC), 1)
     row8 = iota((8, NC), 0) < nz
     for s in range(n_sub):
         tile = st_buf[s, :, wst - NC:wst]
         match = (ccol[...].astype(f32) == tile[nz:nz + 1, :]).astype(f32)
         ct[8 * s:8 * s + 8, :] = dot(jnp.where(row8, tile, 0.0), match, ((1,), (1,)))
+        sc = sc + jnp.sum(match * st_buf[s, nz:nz + 1, 0:NC], axis=1, keepdims=True)
         mine = (ccol[...] == s * own + lane) & (lane < own)
         ws = ws + jnp.sum(jnp.where(mine, tile[nz + 1:nz + 2, :], 0.0), axis=1, keepdims=True)
     wcol[...] = ws
+    scol[...] = sc * ws
     rows_ok = ((iota((blk, wst), 0) & 7) < nz) & (iota((blk, wst), 1) < cm)
     invx[...] = dot(jnp.where(rows_ok, st_buf[...].reshape(blk, wst), 0.0), expand)
 
-    def coarse(k):
-        got = p1_buf[k].reshape(blk, 2 * r_cols)
-        e_all = dot(invx[...], got)
-        e_scr[...] = e_all[:, 0:r_cols]
-        quad = jnp.sum((got * e_all)[:, 0:r_cols], axis=0, keepdims=True)
-        return quad, jnp.sum(p1_buf[k], axis=0)[:, r_cols:2 * r_cols]
-
-    quad, sums = coarse(0)
-    rho_part = sums[0:1, :] + quad
+    def coarse(pieces):
+        e_all = dot(invx[...], pieces)
+        e_scr[...] = e_all
+        return jnp.sum(pieces * e_all, axis=0, keepdims=True)
+
+    rho_part = first_sums[0:1, 0:r_cols] + coarse(first_pieces)
     tz[...] = corner_back(0) + dot(ct[...], e_scr[...], ((0,), (0,)))
     td[...] = tz[...]
     xv[...] = jnp.zeros_like(xv)
 
-    def finish_product(k):
+    def finish_product(k, step, beta):
         sv[0:NC, :] = sv[0:NC, :] + wcol[...] * td[...]
         glue_wait(k, 1)
-        next_left = unpack(k, 1)
-        prev_right = unpack(k, 0)
-        prev_glue = gl_buf[k, 0, hi:hi + 1, 0:r_cols]
-        jump_right = glue_here * (block_of(0) - next_left)
-        jump_left = prev_glue * (prev_right - block_of(1))
+        if k == 0:
+            nlz[...] = unpack(k, 1)
+            prz[...] = unpack(k, 0)
+            nld[...] = nlz[...]
+            prd[...] = prz[...]
+        else:
+            nlz[...] = nlz[...] - step * unpack(k, 1)
+            prz[...] = prz[...] - step * unpack(k, 0)
+            nld[...] = nlz[...] + beta * nld[...]
+            prd[...] = prz[...] + beta * prd[...]
+        prev_glue = gl_buf[0, 0, hi:hi + 1, 0:r_cols]
+        jump_right = glue_here * (block_of(0, dv) - nld[...])
+        jump_left = prev_glue * (prd[...] - block_of(1, dv))
         for b in range(nb):
             rows = slice(NC + b * NI, NC + (b + 1) * NI)
             sv[rows, :] = sv[rows, :] + placed(0, b) * jump_right - placed(1, b) * jump_left
 
-    rho = None
+    rho = step = beta = None
     for k in range(ITERS):
         last = k + 1 == ITERS
-        finish_product(k)
+        finish_product(k, step, beta)
         s, d = sv[...], dv[...]
-        sums = [jnp.sum(d * s, axis=0, keepdims=True)]
+        curve_part = jnp.sum(d * s, axis=0, keepdims=True)
         if not last:
             ds = dmat[...] * s
-            sums.append(jnp.sum(zv[...] * s, axis=0, keepdims=True))
-            sums.append(jnp.sum(ds * s, axis=0, keepdims=True))
+            sums = [
+                curve_part,
+                jnp.sum(zv[...] * s, axis=0, keepdims=True),
+                jnp.sum(ds * s, axis=0, keepdims=True),
+            ]
             first_message(k + 1, s, sums)
             send_first(k + 1)
-            corner_message(k + 1, ds[0:NC, :])
-            send_corners(k + 1)
+            own_corners(k + 1)
+            pieces, sums = first_received(k + 1)
+            quad = coarse(pieces)
+            parts = [sums[0:1, 0:r_cols], sums[1:2, 0:r_cols], sums[0:1, r_cols:] + quad]
         else:
-            first_message(k + 1, s, sums)
-            send_first(k + 1)
-        drain(p1_buf.at[k + 1], p1_sem.at[k + 1], 1, n_sub)
-        if not last:
-            quad, sums = coarse(k + 1)
-            parts = [sums[0:1], sums[1:2], sums[2:3] + quad]
-        else:
-            sums = jnp.sum(p1_buf[k + 1], axis=0)[:, r_cols:2 * r_cols]
-            parts = [sums[0:1], sums[1:2], sums[2:3]]
+            msg = jnp.concatenate([curve_part, curve_part], axis=1)
+            p1_src[k + 1, 0:1] = msg
+            p1_buf[k + 1, me, 0:1] = msg
+            spread(lambda peer: p1_src.at[k + 1], p1_buf.at[k + 1], p1_sem.at[k + 1],
+                   "sub", me, n_sub, 1)
+            drain(p1_buf.at[k + 1], p1_sem.at[k + 1], 1, n_sub, 1)
+            sums = jnp.sum(p1_buf[k + 1, :, 0:1], axis=0)[:, 0:r_cols]
+            parts = [sums, sums, sums]
         msg = jnp.concatenate(
             [
                 jnp.concatenate([parts[0], parts[1]], axis=1),
@@ -278,14 +327,13 @@
         )
         p2_src[k] = msg
         p2_buf[k, cl] = msg
-        spread(lambda peer: p2_src.at[k], p2_buf.at[k], p2_sem.at[k], "cluster", cl, n_cl)
+        spread(lambda peer: p2_src.at[k], p2_buf.at[k], p2_sem.at[k], "cluster", cl, n_cl, 2)
         if not last:
             e_own = e_scr[pl.ds(8 * me, 8), :]
-            q = ds + dot(bt[...], e_own)
-            qv[...] = q
-            tq[...] = dot(ct[...], e_scr[...], ((0,), (0,)))
-            own_corners(k + 1)
-        drain(p2_buf.at[k], p2_sem.at[k], 1, n_cl)
+            qv[...] = ds + dot(bt[...], e_own)
+            send_glue(k + 1, qv)
+            tq[...] = scol[...] * td[...] + dot(ct[...], e_scr[...], ((0,), (0,)))
+        drain(p2_buf.at[k], p2_sem.at[k], 1, n_cl, 2)
         total = jnp.sum(p2_buf[k], axis=0)
         curve = total[0:1, 0:r_cols]
         if k == 0:
@@ -294,27 +342,27 @@
         if last:
             out_ref[...] = xv[...] + step * dv[...]
             break
-        xv[...] = xv[...] + step * dv[...]
         zs = total[0:1, r_cols:2 * r_cols]
         sq = total[1:2, 0:r_cols]
         rho_next = rho - 2.0 * step * zs + step * (step * sq)
         beta = rho_next / rho
+        d = dv[...]
         z = zv[...] - step * qv[...]
         zv[...] = z
-        dv[...] = z + beta * dv[...]
+        dv[...] = z + beta * d
+        xv[...] = xv[...] + step * d
         rho = rho_next
-        send_glue(k + 1)
-        product()
+        product(k + 1, k + 2 == ITERS)
         tz[...] = tz[...] - step * (tq[...] + corner_back(k + 1))
         td[...] = tz[...] + beta * td[...]
 
     drain(st_buf, st_sem, 0, n_sub)
     for k in range(ITERS + 1):
-        drain(p1_buf.at[k], p1_sem.at[k], 0, n_sub)
+        drain(p1_buf.at[k], p1_sem.at[k], 0, n_sub, 5 if k < ITERS else 1)
     for k in range(ITERS):
         drain(rs_buf.at[k], rs_sem.at[k], 0, n_sub)
         drain(ag_buf.at[k], ag_sem.at[k], 0, n_sub)
-        drain(p2_buf.at[k], p2_sem.at[k], 0, n_cl)
+        drain(p2_buf.at[k], p2_sem.at[k], 0, n_cl, 2)
         glue_wait(k, 0)
 
 
@@ -328,14 +376,30 @@
     wst = -(-(cm + NC) // 128) * 128
     vec = pltpu.VMEM((n_rows, r), f32)
     vmem = pl.BlockSpec(memory_space=pltpu.VMEM)
+    hbm = pl.BlockSpec(memory_space=pltpu.HBM)
+    own = corner_weight.shape[1]
     dma = pltpu.SemaphoreType.DMA
     out = pl.pallas_call(
         functools.partial(kernel, n_sub, n_cl),
         out_shape=jax.ShapeDtypeStruct((n_rows, r), f32),
-        in_specs=[pl.BlockSpec(memory_space=pl.ANY)] + [vmem] * 8,
+        in_specs=[hbm] * 9,
         out_specs=vmem,
         scratch_shapes=[
             pltpu.VMEM((n_rows, n_rows), bf16),
+            pltpu.VMEM((r, n_rows), f32),
+            pltpu.VMEM((1, n_rows), f32),
+            pltpu.VMEM((nz, 1, n_rows), f32),
+            pltpu.VMEM((nz, 1, cm), f32),
+            pltpu.VMEM((1, own), f32),
+            pltpu.VMEM((1, NC), jnp.int32),
+            pltpu.VMEM((1, 2), jnp.int32),
+            pltpu.VMEM((1, 1), jnp.int32),
+            vec,
+            pltpu.VMEM((NI, r), f32),
+            pltpu.VMEM((NI, r), f32),
+            pltpu.VMEM((NI, r), f32),
+            pltpu.VMEM((NI, r), f32),
+            pltpu.VMEM((NC, 1), f32),
             pltpu.VMEM((8, n_rows), f32),
             pltpu.VMEM((n_rows, 8), f32),
             vec, vec, vec, vec, vec, vec,
@@ -362,7 +426,7 @@
             pltpu.VMEM((NC, r), f32),
             pltpu.VMEM((NC, r), f32),
             pltpu.VMEM((NC, r), f32),
-            dma(()),
+            dma((9,)),
             dma((2,)),
             dma((ITERS + 1, 2)),
             dma((ITERS, 2)),
@@ -371,11 +435,11 @@
             dma((ITERS, 2, 2)),
         ],
         compiler_params=pltpu.CompilerParams(
-            collective_id=0, has_side_effects=True, vmem_limit_bytes=48 * 1024 * 1024
+            collective_id=0, has_side_effects=True, vmem_limit_bytes=60 * 1024 * 1024
         ),
     )(
-        schur_block[0, 0], load_cases[0, 0], precond_scale[0], coarse_basis[0, 0],
-        coarse_inverse[0], corner_weight, corner_index[0], iface_block[0], glue_link,
+        schur_block[0, 0], load_cases[0, 0].T, precond_scale[0], jnp.swapaxes(coarse_basis[0], 0, 1),
+        jnp.swapaxes(coarse_inverse, 0, 1), corner_weight, corner_index[0], iface_block[0], glue_link,
     )
     return out[None, None]
 

time: 97.8 us -> 88 us (0.90)
  local copies, waits for them, and re-layouts: 7.71 us -> 1.93 us
  Pallas kernels: 89.1 us -> 85.3 us
    unnamed x13 -> x0, local copies, waits for them, and re-layouts: 6.82 us -> none
    pallas_call x1, Pallas kernels: 89.1 us -> 85.3 us  [per_device(): pl.pallas_call(functools.partial(kernel, n_sub, n_cl), out_shape=jax.Shap...]
    broadcast_in_dim x1, local copies, waits for them, and re-layouts: 0.89 us -> 1.93 us  [per_device(): return out[None, None]]
where the time goes in v2:
time: 88 us; the launch traced here: 87.8 us
  Pallas kernels  85.3 us (97%)
  local copies, waits for them, and re-layouts  1.93 us (2%)
    pallas_call x1, Pallas kernels, per_device(): pl.pallas_call(functools.partial(kernel, n_sub, n_cl), out_shape=jax.Shap...  85.3 us
    broadcast_in_dim x1, local copies, waits for them, and re-layouts, per_device(): return out[None, None]  1.93 us

profile of v2, /device:TPU:1, one launch (start us, length us, event | category | flops | bytes accessed | tf_op | source)
XLA Modules:
  0.0 87.8 jit_solution(3934873439067260334)
XLA Ops:
  0.7 85.3 %shard_map.91 = f32[1024,64]{1,0:T(8,128)} custom-call(bf16[1024,1024]{1,0:T(8,128)(2,1)} %bitcast.10, f32[64,1024]{1,0:T(8,128)} %bitcast.12, f32[1,1024]{1,0:T(1,128)} %bitcast.15, f32[6,1,1024]{2,1,0:T(1,128)} %bitcast.13, f32[6,1,192]{2,1,0:T(1,128)} %bitcast.14, f32[1,16]{1,0:T(1,128)} %weight_hbm.1, s32[1,64]{1,0:T(1,128)} %bitcast.16, ...), custom_call_target="tpu_custom_call" | custom-call | tf_op jit(solution)/shard_map/pallas_call | solution.py:382
  85.9 1.9 %copy.10 = f32[1,1,1024,64]{2,3,1,0:T(8,128)} copy(f32[1,1,1024,64]{3,2,1,0:T(8,128)} %bitcast.11) | data formatting | bytes 524288 | tf_op jit(solution)/shard_map/broadcast_in_dim | solution.py:444

commit v3 on v2

--- a/solution.py
+++ b/solution.py
@@ -14,10 +14,25 @@
 bf16 = jnp.bfloat16
 
 
-def dot(a, b, dims=((1,), (0,))):
-    return lax.dot_general(
-        a, b, (dims, ((), ())), precision=lax.Precision.HIGHEST, preferred_element_type=f32
-    )
+def mm(a, b, dims=((1,), (0,))):
+    return lax.dot_general(a, b, (dims, ((), ())), preferred_element_type=f32)
+
+
+def split(x):
+    high = x.astype(bf16)
+    return high, (x - high.astype(f32)).astype(bf16)
+
+
+def split_rows(x):
+    high, low = split(x)
+    return jnp.concatenate([high.astype(f32), low.astype(f32)], axis=0).astype(bf16)
+
+
+def halves_dot(pair, x):
+    n = pair.shape[0] // 2
+    high, low = split(x)
+    both = mm(pair, high)
+    return both[0:n] + both[n:2 * n] + mm(pair[0:n], low)
 
 
 def iota(shape, dim):
@@ -31,7 +46,7 @@
     smat, loads_t, scale_ref, basis_ref, inv_ref, weight_ref, corner_ref, iface_ref, glue_ref,
     lv, nld, prd, nlz, prz, scol,
     b8, bt, dmat, zv, dv, xv, sv, qv,
-    ohT, oh, ct, invx, inv_own, e_scr, ccol, wcol,
+    ohT, oh, ct, ctt, invx, inv_own, grow, e_scr, ccol, wcol,
     st_src, st_buf,
     p1_src, p1_buf, rs_src, rs_buf, ag_src, ag_buf, p2_src, p2_buf, gl_src, gl_buf,
     tq, td, tz,
@@ -85,52 +100,64 @@
 
     for copy in copies[:-1]:
         copy.wait()
-    for i in range(nz):
-        b8[i:i + 1, :] = basis_ref[i]
-    b8[nz:nz + 1, :] = scale_ref[...]
-    b8[nz + 1:8, :] = jnp.zeros((7 - nz, n_rows), f32)
-    bt[...] = jnp.transpose(b8[...])
-    pick = ((iota((8, r_cols), 0) == nz)).astype(f32)
-    dmat[...] = dot(bt[...], pick)
-    b8[nz:nz + 1, :] = jnp.zeros((1, n_rows), f32)
+    basis8 = jnp.concatenate([basis_ref[i] for i in range(nz)] + [jnp.zeros((8 - nz, n_rows), f32)], axis=0)
+    b8[...] = split_rows(basis8)
+    high, low = split(basis8)
+    high, low = high.astype(f32), low.astype(f32)
+    cols = jnp.transpose(
+        jnp.concatenate([high, high, low, jnp.broadcast_to(scale_ref[...], (8, n_rows))], axis=0)
+    )
+    bt[...] = cols.astype(bf16)
+    dmat[...] = jnp.broadcast_to(cols[:, 24:25], (n_rows, r_cols))
 
     corner_row = corner_ref[...]
     eye = iota((NC, NC), 0) == iota((NC, NC), 1)
-    ccol[...] = jnp.sum(jnp.where(eye, corner_row, 0), axis=1, keepdims=True)
+    ccol[...] = jnp.sum(jnp.where(eye, corner_row, 0), axis=1, keepdims=True).astype(f32)
+    corner_col = ccol[...].astype(jnp.int32)
 
     m = iota((blk, NC), 0)
     base = (m >> 3) * own + (m & 7)
-    oh[:, 0:NC] = (base == corner_row).astype(f32)
-    oh[:, NC:2 * NC] = (base + half == corner_row).astype(f32)
+    first, second = (base == corner_row).astype(f32), (base + half == corner_row).astype(f32)
+    oh[...] = jnp.concatenate([first, second, first, second], axis=1).astype(bf16)
     m = iota((NC, blk), 1)
     base = (m >> 3) * own + (m & 7)
-    ohT[0:NC, :] = (base == ccol[...]).astype(f32)
-    ohT[NC:2 * NC, :] = (base + half == ccol[...]).astype(f32)
+    pick = jnp.concatenate([base == corner_col, base + half == corner_col], axis=0)
+    pick = pick.astype(f32).astype(bf16)
+    ohT[...] = jnp.concatenate([pick, pick], axis=1)
 
     st_src[...] = jnp.zeros(st_src.shape, f32)
     for i in range(nz):
         st_src[i:i + 1, 0:cm] = inv_ref[i]
-    st_src[0:nz, wst - NC:wst] = b8[0:nz, 0:NC]
-    st_src[nz:nz + 1, 0:NC] = scale_ref[:, 0:NC]
-    st_src[nz:nz + 1, wst - NC:wst] = corner_row.astype(f32)
-    st_src[nz + 1:nz + 2, wst - NC:wst - NC + own] = weight_ref[...]
+    st_src[0:nz, wst - NC:wst] = basis8[0:nz, 0:NC]
+    st_src[nz:nz + 1, wst - NC:wst] = scale_ref[:, 0:NC]
+    st_src[nz + 1:nz + 2, wst - NC:wst] = corner_row.astype(f32)
+    st_src[nz + 1:nz + 2, 0:own] = weight_ref[...]
 
     ea, eb = iota((wst, blk), 0), iota((wst, blk), 1)
-    expand = ((ea == (eb >> 3) * nz + (eb & 7)) & ((eb & 7) < nz) & (ea < cm)).astype(f32)
+    grow[...] = (
+        ((ea == (eb >> 3) * nz + (eb & 7)) & ((eb & 7) < nz) & (ea < cm)).astype(f32).astype(bf16)
+    )
     row_ok = iota((8, wst), 0) < nz
-    inv_own[...] = dot(jnp.where(row_ok, st_src[...], 0.0), expand)
+    inv_own[...] = mm(split_rows(jnp.where(row_ok, st_src[...], 0.0)), grow[...]).astype(bf16)
 
     def packed_corners(v):
-        z = jnp.zeros((NC, r_cols), f32)
-        vv = jnp.concatenate(
-            [jnp.concatenate([v, z], axis=1), jnp.concatenate([z, v], axis=1)], axis=0
-        )
-        return dot(oh[...], vv)
+        zero = jnp.zeros((NC, r_cols), f32)
+        parts = []
+        for x in split(v):
+            x = x.astype(f32)
+            parts += [jnp.concatenate([x, zero], axis=1), jnp.concatenate([zero, x], axis=1)]
+        return mm(oh[...], jnp.concatenate(parts, axis=0).astype(bf16))
+
+    def basis_t(e):
+        high, low = split(e)
+        high, low = high.astype(f32), low.astype(f32)
+        stack = jnp.concatenate([high, low, high, jnp.zeros((8, r_cols), f32)], axis=0)
+        return mm(bt[...], stack.astype(bf16))
 
     tail = jnp.zeros((3, r_cols), f32)
 
     def first_message(k, vec, sums):
-        pieces = dot(b8[...], vec)
+        pieces = halves_dot(b8[...], vec)
         sums = list(sums) + [jnp.zeros((1, r_cols), f32)] * (4 - len(sums))
         msg = jnp.concatenate(
             [
@@ -171,7 +198,8 @@
     def corner_back(k):
         drain(ag_buf.at[k], ag_sem.at[k], 1, n_sub)
         got = ag_buf[k].reshape(blk, 2 * r_cols)
-        quad = dot(ohT[...], got)
+        high, low = split(got)
+        quad = mm(ohT[...], jnp.concatenate([high, low], axis=0))
         return quad[0:NC, 0:r_cols] + quad[NC:2 * NC, r_cols:2 * r_cols]
 
     glue_here = glue_ref[...].astype(f32)
@@ -210,23 +238,45 @@
         a = gl_buf[k, side, 0:hi, :]
         return jnp.concatenate([a[:, 0:r_cols], a[:, r_cols:2 * r_cols]], axis=0)
 
+    def spread_static():
+        @pl.loop(1, n_sub // 2)
+        def _(i):
+            pltpu.make_async_remote_copy(
+                src_ref=st_src,
+                dst_ref=st_buf.at[core, place],
+                send_sem=st_sem.at[0],
+                recv_sem=st_sem.at[1],
+                device_id={"sub": lax.rem(me + 2 * i, n_sub)},
+            ).start()
+
+    def pair_static():
+        view = st_buf.at[0, pl.ds(0, n_sub // 2 - 1)]
+        pltpu.make_async_copy(view, view, st_sem.at[1]).wait()
+        pltpu.make_async_remote_copy(
+            src_ref=st_buf.at[core],
+            dst_ref=st_buf.at[core],
+            send_sem=st_sem.at[2],
+            recv_sem=st_sem.at[3],
+            device_id={"sub": me + 1 - 2 * core},
+        ).start()
+
     lv[...] = jnp.transpose(loads_t[...])
     loads = lv[...]
     scaled = dmat[...] * loads
     corner_message(0, scaled[0:NC, :])
     first_message(0, loads, [jnp.sum(scaled * loads, axis=0, keepdims=True)])
-    st_buf[me] = st_src[...]
+    core, place = lax.rem(me, 2), lax.div(me, 2)
+    st_buf[core, place] = st_src[...]
 
     pl.semaphore_wait(barrier, n_sub + n_cl - 2)
 
     send_corners(0)
     send_first(0)
-    spread(lambda peer: st_src, st_buf, st_sem, "sub", me, n_sub)
+    spread_static()
     copies[-1].wait()
     own_corners(0)
     first_pieces, first_sums = first_received(0)
-    e_own = dot(inv_own[...], first_pieces)
-    z = dmat[...] * lv[...] + dot(bt[...], e_own * (iota((8, r_cols), 0) < nz).astype(f32))
+    z = dmat[...] * lv[...] + basis_t(halves_dot(inv_own[...], first_pieces))
     zv[...] = z
     dv[...] = z
 
@@ -243,30 +293,37 @@
 
     product(0, False)
 
-    drain(st_buf, st_sem, 1, n_sub)
-    ws = jnp.zeros((NC, 1), f32)
-    sc = jnp.zeros((NC, 1), f32)
-    lane = iota((NC, NC), 1)
-    row8 = iota((8, NC), 0) < nz
+    pair_static()
+    pltpu.make_async_copy(st_buf.at[0], st_buf.at[0], st_sem.at[3]).wait()
+    ws = jnp.zeros((NC, NC), f32)
+    srow = jnp.zeros((1, NC), f32)
+    lane = iota((NC, NC), 1).astype(f32)
     for s in range(n_sub):
-        tile = st_buf[s, :, wst - NC:wst]
-        match = (ccol[...].astype(f32) == tile[nz:nz + 1, :]).astype(f32)
-        ct[8 * s:8 * s + 8, :] = dot(jnp.where(row8, tile, 0.0), match, ((1,), (1,)))
-        sc = sc + jnp.sum(match * st_buf[s, nz:nz + 1, 0:NC], axis=1, keepdims=True)
-        mine = (ccol[...] == s * own + lane) & (lane < own)
-        ws = ws + jnp.sum(jnp.where(mine, tile[nz + 1:nz + 2, :], 0.0), axis=1, keepdims=True)
-    wcol[...] = ws
-    scol[...] = sc * ws
-    rows_ok = ((iota((blk, wst), 0) & 7) < nz) & (iota((blk, wst), 1) < cm)
-    invx[...] = dot(jnp.where(rows_ok, st_buf[...].reshape(blk, wst), 0.0), expand)
+        slot = st_buf[s % 2, s // 2]
+        tile = slot[:, wst - NC:wst]
+        match = (ccol[...] == tile[nz + 1:nz + 2, :]).astype(f32).astype(bf16)
+        both = mm(split_rows(tile), match, ((1,), (1,)))
+        rows = both[0:8] + both[8:16]
+        ct[8 * s:8 * s + 8, :] = rows
+        srow = srow + rows[nz:nz + 1, :]
+        mine = (ccol[...] - float(s) * own == lane) & (lane < own)
+        ws = ws + jnp.where(mine, slot[nz + 1:nz + 2, 0:NC], 0.0)
+    wcol[...] = jnp.sum(ws, axis=1, keepdims=True)
+    scol[...] = jnp.sum(jnp.where(eye, srow, 0.0), axis=1, keepdims=True) * wcol[...]
+    ctt[...] = split_rows(jnp.transpose(ct[...]))
+    row_ok = (iota((8, wst), 0) < nz) & (iota((8, wst), 1) < cm)
+    stacked = jnp.concatenate(
+        [jnp.where(row_ok, st_buf[s % 2, s // 2], 0.0) for s in range(n_sub)], axis=0
+    )
+    invx[...] = mm(split_rows(stacked), grow[...]).astype(bf16)
 
     def coarse(pieces):
-        e_all = dot(invx[...], pieces)
+        e_all = halves_dot(invx[...], pieces)
         e_scr[...] = e_all
         return jnp.sum(pieces * e_all, axis=0, keepdims=True)
 
     rho_part = first_sums[0:1, 0:r_cols] + coarse(first_pieces)
-    tz[...] = corner_back(0) + dot(ct[...], e_scr[...], ((0,), (0,)))
+    tz[...] = corner_back(0) + halves_dot(ctt[...], e_scr[...])
     td[...] = tz[...]
     xv[...] = jnp.zeros_like(xv)
 
@@ -330,9 +387,9 @@
         spread(lambda peer: p2_src.at[k], p2_buf.at[k], p2_sem.at[k], "cluster", cl, n_cl, 2)
         if not last:
             e_own = e_scr[pl.ds(8 * me, 8), :]
-            qv[...] = ds + dot(bt[...], e_own)
+            qv[...] = ds + basis_t(e_own)
             send_glue(k + 1, qv)
-            tq[...] = scol[...] * td[...] + dot(ct[...], e_scr[...], ((0,), (0,)))
+            tq[...] = scol[...] * td[...] + halves_dot(ctt[...], e_scr[...])
         drain(p2_buf.at[k], p2_sem.at[k], 1, n_cl, 2)
         total = jnp.sum(p2_buf[k], axis=0)
         curve = total[0:1, 0:r_cols]
@@ -356,7 +413,9 @@
         tz[...] = tz[...] - step * (tq[...] + corner_back(k + 1))
         td[...] = tz[...] + beta * td[...]
 
-    drain(st_buf, st_sem, 0, n_sub)
+    view = st_buf.at[0, pl.ds(0, n_sub // 2 - 1)]
+    pltpu.make_async_copy(view, view, st_sem.at[0]).wait()
+    pltpu.make_async_copy(st_buf.at[0], st_buf.at[0], st_sem.at[2]).wait()
     for k in range(ITERS + 1):
         drain(p1_buf.at[k], p1_sem.at[k], 0, n_sub, 5 if k < ITERS else 1)
     for k in range(ITERS):
@@ -400,19 +459,21 @@
             pltpu.VMEM((NI, r), f32),
             pltpu.VMEM((NI, r), f32),
             pltpu.VMEM((NC, 1), f32),
-            pltpu.VMEM((8, n_rows), f32),
-            pltpu.VMEM((n_rows, 8), f32),
+            pltpu.VMEM((16, n_rows), bf16),
+            pltpu.VMEM((n_rows, 32), bf16),
             vec, vec, vec, vec, vec, vec,
-            pltpu.VMEM((2 * NC, blk), f32),
-            pltpu.VMEM((blk, 2 * NC), f32),
+            pltpu.VMEM((2 * NC, 2 * blk), bf16),
+            pltpu.VMEM((blk, 4 * NC), bf16),
             pltpu.VMEM((blk, NC), f32),
-            pltpu.VMEM((blk, blk), f32),
-            pltpu.VMEM((8, blk), f32),
+            pltpu.VMEM((2 * NC, blk), bf16),
+            pltpu.VMEM((2 * blk, blk), bf16),
+            pltpu.VMEM((16, blk), bf16),
+            pltpu.VMEM((wst, blk), bf16),
             pltpu.VMEM((blk, r), f32),
-            pltpu.VMEM((NC, 1), jnp.int32),
+            pltpu.VMEM((NC, 1), f32),
             pltpu.VMEM((NC, 1), f32),
             pltpu.VMEM((8, wst), f32),
-            pltpu.VMEM((n_sub, 8, wst), f32),
+            pltpu.VMEM((2, n_sub // 2, 8, wst), f32),
             pltpu.VMEM((ITERS + 1, 8, 2 * r), f32),
             pltpu.VMEM((ITERS + 1, n_sub, 8, 2 * r), f32),
             pltpu.VMEM((ITERS, n_sub, 8, 2 * r), f32),
@@ -427,7 +488,7 @@
             pltpu.VMEM((NC, r), f32),
             pltpu.VMEM((NC, r), f32),
             dma((9,)),
-            dma((2,)),
+            dma((4,)),
             dma((ITERS + 1, 2)),
             dma((ITERS, 2)),
             dma((ITERS, 2)),
@@ -435,7 +496,7 @@
             dma((ITERS, 2, 2)),
         ],
         compiler_params=pltpu.CompilerParams(
-            collective_id=0, has_side_effects=True, vmem_limit_bytes=60 * 1024 * 1024
+            collective_id=0, has_side_effects=True, vmem_limit_bytes=40 * 1024 * 1024
         ),
     )(
         schur_block[0, 0], load_cases[0, 0].T, precond_scale[0], jnp.swapaxes(coarse_basis[0], 0, 1),

time: 88 us -> 83 us (0.943)
  Pallas kernels: 85.3 us -> 74.5 us
  local copies, waits for them, and re-layouts: 1.93 us -> 7.5 us
    pallas_call x1, Pallas kernels: 85.3 us -> 74.5 us  [per_device(): pl.pallas_call(functools.partial(kernel, n_sub, n_cl), out_shape=jax.Shap...]
    unnamed x0 -> x16, local copies, waits for them, and re-layouts: none -> 6.61 us
    broadcast_in_dim x1, local copies, waits for them, and re-layouts: 1.93 us -> 0.89 us  [per_device(): return out[None, None]]
where the time goes in v3:
time: 83 us; the launch traced here: 82.7 us
  Pallas kernels  74.5 us (90%)
  local copies, waits for them, and re-layouts  7.5 us (9%)
    pallas_call x1, Pallas kernels, per_device(): pl.pallas_call(functools.partial(kernel, n_sub, n_cl), out_shape=jax.Shap...  74.5 us
    unnamed x16, local copies, waits for them, and re-layouts  6.61 us

profile of v3, /device:TPU:1, one launch (start us, length us, event | category | flops | bytes accessed | tf_op | source)
XLA Modules:
  0.0 82.7 jit_solution(5423698209991405714)
XLA Ops:
  0.7 0.0 copy-start
  0.7 1.6 %copy-done = bf16[1,1,1024,1024]{3,2,1,0:T(8,128)(2,1)S(1)} copy-done((bf16[1,1,1024,1024]{3,2,1,0:T(8,128)(2,1)S(1)}, bf16[1,1,1024,1024]{3,2,1,0:T(8,128)(2,1)}, u32[]{:S(2)}) %copy-start) | copy-done | bytes 2097176
  2.2 0.0 copy-start.1
  2.2 0.9 %copy-done.1 = f32[1,1,1024,64]{2,3,1,0:T(8,128)S(1)} copy-done((f32[1,1,1024,64]{2,3,1,0:T(8,128)S(1)}, f32[1,1,1024,64]{2,3,1,0:T(8,128)}, u32[]{:S(2)}) %copy-start.1) | copy-done | bytes 262168
  3.2 0.0 copy-start.2
  3.2 0.7 copy-done.2
  3.9 0.0 copy-start.3
  3.9 0.7 copy-done.3
  4.6 0.0 copy-start.4
  4.6 0.7 copy-done.4
  5.3 0.0 copy-start.5
  5.3 0.7 copy-done.5
  6.0 0.0 copy-start.6
  6.0 0.7 copy-done.6
  6.6 0.0 copy-start.7
  6.6 0.7 copy-done.7
  7.3 74.5 %shard_map.91 = f32[1024,64]{1,0:T(8,128)S(1)} custom-call(bf16[1024,1024]{1,0:T(8,128)(2,1)S(1)} %bitcast.10, f32[64,1024]{1,0:T(8,128)S(1)} %bitcast.12, f32[1,1024]{1,0:T(1,128)S(1)} %bitcast.15, f32[6,1,1024]{2,1,0:T(1,128)S(1)} %bitcast.13, f32[6,1,192]{2,1,0:T(1,128)S(1)} %bitcast.14, f32[1,16]{1,0:T(1,128)S(1)} %copy-done.5, s32[1,64]{1,0:T(1,128)S(1)} %bitcast.16, ...), custom_call_target="tpu_custom_call" | custom-call | tf_op jit(solution)/shard_map/pallas_call | solution.py:441
  81.8 0.9 %copy.10 = f32[1,1,1024,64]{2,3,1,0:T(8,128)} copy(f32[1,1,1024,64]{3,2,1,0:T(8,128)S(1)} %bitcast.11) | data formatting | bytes 524288 | tf_op jit(solution)/shard_map/broadcast_in_dim | solution.py:505
Async XLA Ops:
  0.7 1.6 %copy-start = (bf16[1,1,1024,1024]{3,2,1,0:T(8,128)(2,1)S(1)}, bf16[1,1,1024,1024]{3,2,1,0:T(8,128)(2,1)}, u32[]{:S(2)}) copy-start(bf16[1,1,1024,1024]{3,2,1,0:T(8,128)(2,1)} %param.9) | copy-start | bytes 6291460
  2.2 0.9 %copy-start.1 = (f32[1,1,1024,64]{2,3,1,0:T(8,128)S(1)}, f32[1,1,1024,64]{2,3,1,0:T(8,128)}, u32[]{:S(2)}) copy-start(f32[1,1,1024,64]{2,3,1,0:T(8,128)} %param.10) | copy-start | bytes 786436
  3.2 0.7 copy-start.2
  3.9 0.7 copy-start.3
  4.6 0.7 copy-start.4
  5.3 0.7 copy-start.5
  6.0 0.7 copy-start.6
  6.6 0.7 copy-start.7

commit v4 on v3

--- a/solution.py
+++ b/solution.py
@@ -46,7 +46,7 @@
     smat, loads_t, scale_ref, basis_ref, inv_ref, weight_ref, corner_ref, iface_ref, glue_ref,
     lv, nld, prd, nlz, prz, scol,
     b8, bt, dmat, zv, dv, xv, sv, qv,
-    ohT, oh, ct, ctt, invx, inv_own, grow, e_scr, ccol, wcol,
+    ohT, oh, ct, ctt, wide, invx, inv_own, grow, e_scr, ccol, wcol,
     st_src, st_buf,
     p1_src, p1_buf, rs_src, rs_buf, ag_src, ag_buf, p2_src, p2_buf, gl_src, gl_buf,
     tq, td, tz,
@@ -293,29 +293,39 @@
 
     product(0, False)
 
+    lane = iota((NC, NC), 1).astype(f32)
+    row_ok = (iota((8, wst), 0) < nz) & (iota((8, wst), 1) < cm)
+    n_half = n_sub // 2
+
+    def tables(side, ws, srow):
+        stack = []
+        for i in range(n_half):
+            slot = st_buf[side, i]
+            tile = slot[:, wst - NC:wst]
+            match = (ccol[...] == tile[nz + 1:nz + 2, :]).astype(f32).astype(bf16)
+            both = mm(split_rows(tile), match, ((1,), (1,)))
+            rows = both[0:8] + both[8:16]
+            s = 2 * i + side
+            ct[pl.ds(pl.multiple_of(8 * s, 8), 8), :] = rows
+            srow = srow + rows[nz:nz + 1, :]
+            mine = (ccol[...] - (s * own).astype(f32) == lane) & (lane < own)
+            ws = ws + jnp.where(mine, slot[nz + 1:nz + 2, 0:NC], 0.0)
+            stack.append(jnp.where(row_ok, slot, 0.0))
+        both = mm(split_rows(jnp.concatenate(stack, axis=0)), grow[...])
+        for i in range(n_half):
+            row = pl.multiple_of(8 * (2 * i + side), 8)
+            wide[pl.ds(row, 8), :] = both[8 * i:8 * i + 8]
+            wide[pl.ds(blk + row, 8), :] = both[8 * (n_half + i):8 * (n_half + i) + 8]
+        return ws, srow
+
     pair_static()
+    ws, srow = tables(core, jnp.zeros((NC, NC), f32), jnp.zeros((1, NC), f32))
     pltpu.make_async_copy(st_buf.at[0], st_buf.at[0], st_sem.at[3]).wait()
-    ws = jnp.zeros((NC, NC), f32)
-    srow = jnp.zeros((1, NC), f32)
-    lane = iota((NC, NC), 1).astype(f32)
-    for s in range(n_sub):
-        slot = st_buf[s % 2, s // 2]
-        tile = slot[:, wst - NC:wst]
-        match = (ccol[...] == tile[nz + 1:nz + 2, :]).astype(f32).astype(bf16)
-        both = mm(split_rows(tile), match, ((1,), (1,)))
-        rows = both[0:8] + both[8:16]
-        ct[8 * s:8 * s + 8, :] = rows
-        srow = srow + rows[nz:nz + 1, :]
-        mine = (ccol[...] - float(s) * own == lane) & (lane < own)
-        ws = ws + jnp.where(mine, slot[nz + 1:nz + 2, 0:NC], 0.0)
+    ws, srow = tables(1 - core, ws, srow)
     wcol[...] = jnp.sum(ws, axis=1, keepdims=True)
     scol[...] = jnp.sum(jnp.where(eye, srow, 0.0), axis=1, keepdims=True) * wcol[...]
     ctt[...] = split_rows(jnp.transpose(ct[...]))
-    row_ok = (iota((8, wst), 0) < nz) & (iota((8, wst), 1) < cm)
-    stacked = jnp.concatenate(
-        [jnp.where(row_ok, st_buf[s % 2, s // 2], 0.0) for s in range(n_sub)], axis=0
-    )
-    invx[...] = mm(split_rows(stacked), grow[...]).astype(bf16)
+    invx[...] = wide[...].astype(bf16)
 
     def coarse(pieces):
         e_all = halves_dot(invx[...], pieces)
@@ -438,6 +448,11 @@
     hbm = pl.BlockSpec(memory_space=pltpu.HBM)
     own = corner_weight.shape[1]
     dma = pltpu.SemaphoreType.DMA
+    operands = (
+        schur_block[0, 0], load_cases[0, 0].T, precond_scale[0],
+        jnp.swapaxes(coarse_basis[0], 0, 1), jnp.swapaxes(coarse_inverse, 0, 1),
+        corner_weight, corner_index[0], iface_block[0],
+    )
     out = pl.pallas_call(
         functools.partial(kernel, n_sub, n_cl),
         out_shape=jax.ShapeDtypeStruct((n_rows, r), f32),
@@ -466,6 +481,7 @@
             pltpu.VMEM((blk, 4 * NC), bf16),
             pltpu.VMEM((blk, NC), f32),
             pltpu.VMEM((2 * NC, blk), bf16),
+            pltpu.VMEM((2 * blk, blk), f32),
             pltpu.VMEM((2 * blk, blk), bf16),
             pltpu.VMEM((16, blk), bf16),
             pltpu.VMEM((wst, blk), bf16),
@@ -499,8 +515,7 @@
             collective_id=0, has_side_effects=True, vmem_limit_bytes=40 * 1024 * 1024
         ),
     )(
-        schur_block[0, 0], load_cases[0, 0].T, precond_scale[0], jnp.swapaxes(coarse_basis[0], 0, 1),
-        jnp.swapaxes(coarse_inverse, 0, 1), corner_weight, corner_index[0], iface_block[0], glue_link,
+        *(pltpu.with_memory_space_constraint(a, pltpu.HBM) for a in operands), glue_link,
     )
     return out[None, None]
 

time: 83 us -> 76.6 us (0.923)
  local copies, waits for them, and re-layouts: 7.5 us -> 0.89 us
    unnamed x16 -> x0, local copies, waits for them, and re-layouts: 6.61 us -> none
where the time goes in v4:
time: 76.6 us; the launch traced here: 76.4 us
  Pallas kernels  74.9 us (98%)
  local copies, waits for them, and re-layouts  0.89 us (1%)
    pallas_call x1, Pallas kernels, per_device(): pl.pallas_call(functools.partial(kernel, n_sub, n_cl), out_shape=jax.Shap...  74.9 us

profile of v4, /device:TPU:1, one launch (start us, length us, event | category | flops | bytes accessed | tf_op | source)
XLA Modules:
  0.0 76.4 jit_solution(1061640956168780893)
XLA Ops:
  0.7 74.9 %shard_map.91 = f32[1024,64]{1,0:T(8,128)S(1)} custom-call(bf16[1024,1024]{1,0:T(8,128)(2,1)} %bitcast.11, f32[64,1024]{1,0:T(8,128)} %bitcast.12, f32[1,1024]{1,0:T(1,128)} %bitcast.15, f32[6,1,1024]{2,1,0:T(1,128)} %bitcast.13, f32[6,1,192]{2,1,0:T(1,128)} %bitcast.14, f32[1,16]{1,0:T(1,128)} %weight_hbm.1, s32[1,64]{1,0:T(1,128)} %bitcast.16, ...), custom_call_target="tpu_custom_call" | custom-call | tf_op jit(solution)/shard_map/pallas_call | solution.py:456
  75.5 0.9 %copy.10 = f32[1,1,1024,64]{2,3,1,0:T(8,128)} copy(f32[1,1,1024,64]{3,2,1,0:T(8,128)S(1)} %bitcast.10) | data formatting | bytes 524288 | tf_op jit(solution)/shard_map/broadcast_in_dim | solution.py:520

commit v5 on v4

--- a/solution.py
+++ b/solution.py
@@ -130,8 +130,8 @@
         st_src[i:i + 1, 0:cm] = inv_ref[i]
     st_src[0:nz, wst - NC:wst] = basis8[0:nz, 0:NC]
     st_src[nz:nz + 1, wst - NC:wst] = scale_ref[:, 0:NC]
-    st_src[nz + 1:nz + 2, wst - NC:wst] = corner_row.astype(f32)
-    st_src[nz + 1:nz + 2, 0:own] = weight_ref[...]
+    st_src[nz:nz + 1, NC:2 * NC] = corner_row.astype(f32)
+    st_src[nz:nz + 1, 0:own] = weight_ref[...]
 
     ea, eb = iota((wst, blk), 0), iota((wst, blk), 1)
     grow[...] = (
@@ -242,19 +242,19 @@
         @pl.loop(1, n_sub // 2)
         def _(i):
             pltpu.make_async_remote_copy(
-                src_ref=st_src,
-                dst_ref=st_buf.at[core, place],
+                src_ref=st_src.at[pl.ds(0, 7)],
+                dst_ref=st_buf.at[core, place, pl.ds(0, 7)],
                 send_sem=st_sem.at[0],
                 recv_sem=st_sem.at[1],
                 device_id={"sub": lax.rem(me + 2 * i, n_sub)},
             ).start()
 
     def pair_static():
-        view = st_buf.at[0, pl.ds(0, n_sub // 2 - 1)]
+        view = st_buf.at[0, pl.ds(0, n_sub // 2 - 1), pl.ds(0, 7)]
         pltpu.make_async_copy(view, view, st_sem.at[1]).wait()
         pltpu.make_async_remote_copy(
-            src_ref=st_buf.at[core],
-            dst_ref=st_buf.at[core],
+            src_ref=st_buf.at[core, :, pl.ds(0, 7)],
+            dst_ref=st_buf.at[core, :, pl.ds(0, 7)],
             send_sem=st_sem.at[2],
             recv_sem=st_sem.at[3],
             device_id={"sub": me + 1 - 2 * core},
@@ -280,65 +280,7 @@
     zv[...] = z
     dv[...] = z
 
-    def product(k, last):
-        half_d = dv[...].astype(bf16)
-        top = jnp.dot(smat[0:NC, :], half_d, preferred_element_type=f32)
-        sv[0:NC, :] = top
-        if not last:
-            corner_message(k + 1, dmat[0:NC, :] * top)
-            send_corners(k + 1)
-        if k == 0:
-            send_glue(0, zv)
-        sv[NC:, :] = jnp.dot(smat[NC:, :], half_d, preferred_element_type=f32)
-
-    product(0, False)
-
-    lane = iota((NC, NC), 1).astype(f32)
-    row_ok = (iota((8, wst), 0) < nz) & (iota((8, wst), 1) < cm)
-    n_half = n_sub // 2
-
-    def tables(side, ws, srow):
-        stack = []
-        for i in range(n_half):
-            slot = st_buf[side, i]
-            tile = slot[:, wst - NC:wst]
-            match = (ccol[...] == tile[nz + 1:nz + 2, :]).astype(f32).astype(bf16)
-            both = mm(split_rows(tile), match, ((1,), (1,)))
-            rows = both[0:8] + both[8:16]
-            s = 2 * i + side
-            ct[pl.ds(pl.multiple_of(8 * s, 8), 8), :] = rows
-            srow = srow + rows[nz:nz + 1, :]
-            mine = (ccol[...] - (s * own).astype(f32) == lane) & (lane < own)
-            ws = ws + jnp.where(mine, slot[nz + 1:nz + 2, 0:NC], 0.0)
-            stack.append(jnp.where(row_ok, slot, 0.0))
-        both = mm(split_rows(jnp.concatenate(stack, axis=0)), grow[...])
-        for i in range(n_half):
-            row = pl.multiple_of(8 * (2 * i + side), 8)
-            wide[pl.ds(row, 8), :] = both[8 * i:8 * i + 8]
-            wide[pl.ds(blk + row, 8), :] = both[8 * (n_half + i):8 * (n_half + i) + 8]
-        return ws, srow
-
-    pair_static()
-    ws, srow = tables(core, jnp.zeros((NC, NC), f32), jnp.zeros((1, NC), f32))
-    pltpu.make_async_copy(st_buf.at[0], st_buf.at[0], st_sem.at[3]).wait()
-    ws, srow = tables(1 - core, ws, srow)
-    wcol[...] = jnp.sum(ws, axis=1, keepdims=True)
-    scol[...] = jnp.sum(jnp.where(eye, srow, 0.0), axis=1, keepdims=True) * wcol[...]
-    ctt[...] = split_rows(jnp.transpose(ct[...]))
-    invx[...] = wide[...].astype(bf16)
-
-    def coarse(pieces):
-        e_all = halves_dot(invx[...], pieces)
-        e_scr[...] = e_all
-        return jnp.sum(pieces * e_all, axis=0, keepdims=True)
-
-    rho_part = first_sums[0:1, 0:r_cols] + coarse(first_pieces)
-    tz[...] = corner_back(0) + halves_dot(ctt[...], e_scr[...])
-    td[...] = tz[...]
-    xv[...] = jnp.zeros_like(xv)
-
-    def finish_product(k, step, beta):
-        sv[0:NC, :] = sv[0:NC, :] + wcol[...] * td[...]
+    def jumps(k, step, beta):
         glue_wait(k, 1)
         if k == 0:
             nlz[...] = unpack(k, 1)
@@ -351,16 +293,84 @@
             nld[...] = nlz[...] + beta * nld[...]
             prd[...] = prz[...] + beta * prd[...]
         prev_glue = gl_buf[0, 0, hi:hi + 1, 0:r_cols]
-        jump_right = glue_here * (block_of(0, dv) - nld[...])
-        jump_left = prev_glue * (prd[...] - block_of(1, dv))
+        return glue_here * (block_of(0, dv) - nld[...]), prev_glue * (prd[...] - block_of(1, dv))
+
+    def add_jumps(jump):
         for b in range(nb):
             rows = slice(NC + b * NI, NC + (b + 1) * NI)
-            sv[rows, :] = sv[rows, :] + placed(0, b) * jump_right - placed(1, b) * jump_left
+            sv[rows, :] = sv[rows, :] + placed(0, b) * jump[0] - placed(1, b) * jump[1]
+
+    def product(k, last, step, beta):
+        half_d = dv[...].astype(bf16)
+        top = mm(smat[0:NC, :], half_d)
+        sv[0:NC, :] = top
+        if not last:
+            corner_message(k + 1, dmat[0:NC, :] * top)
+        if k == 0:
+            send_glue(0, zv)
+        elif not last:
+            send_corners(k + 1)
+        if k > 0:
+            jump = jumps(k, step, beta)
+        sv[NC:, :] = mm(smat[NC:, :], half_d)
+        if k > 0:
+            add_jumps(jump)
+
+    product(0, False, None, None)
+
+    lane = iota((NC, NC), 1).astype(f32)
+    row_ok = (iota((8, wst), 0) < nz) & (iota((8, wst), 1) < cm)
+    tile_ok = iota((8, NC), 0) <= nz
+    n_half = n_sub // 2
+
+    def tables(side, ws, srow):
+        stack = []
+        for i in range(n_half):
+            slot = st_buf[side, i]
+            tile = jnp.where(tile_ok, slot[:, wst - NC:wst], 0.0)
+            match = (ccol[...] == slot[nz:nz + 1, NC:2 * NC]).astype(f32).astype(bf16)
+            both = mm(split_rows(tile), match, ((1,), (1,)))
+            rows = both[0:8] + both[8:16]
+            s = 2 * i + side
+            ct[pl.ds(pl.multiple_of(8 * s, 8), 8), :] = rows
+            srow = srow + rows[nz:nz + 1, :]
+            mine = (ccol[...] - (s * own).astype(f32) == lane) & (lane < own)
+            ws = ws + jnp.where(mine, slot[nz:nz + 1, 0:NC], 0.0)
+            stack.append(jnp.where(row_ok, slot, 0.0))
+        both = mm(split_rows(jnp.concatenate(stack, axis=0)), grow[...])
+        for i in range(n_half):
+            row = pl.multiple_of(8 * (2 * i + side), 8)
+            wide[pl.ds(row, 8), :] = both[8 * i:8 * i + 8]
+            wide[pl.ds(blk + row, 8), :] = both[8 * (n_half + i):8 * (n_half + i) + 8]
+        return ws, srow
+
+    pair_static()
+    send_corners(1)
+    ws, srow = tables(core, jnp.zeros((NC, NC), f32), jnp.zeros((1, NC), f32))
+    view = st_buf.at[0, :, pl.ds(0, 7)]
+    pltpu.make_async_copy(view, view, st_sem.at[3]).wait()
+    ws, srow = tables(1 - core, ws, srow)
+    wcol[...] = jnp.sum(ws, axis=1, keepdims=True)
+    scol[...] = jnp.sum(jnp.where(eye, srow, 0.0), axis=1, keepdims=True) * wcol[...]
+    ctt[...] = split_rows(jnp.transpose(ct[...]))
+    invx[...] = wide[...].astype(bf16)
+
+    def coarse(pieces):
+        e_all = halves_dot(invx[...], pieces)
+        e_scr[...] = e_all
+        return jnp.sum(pieces * e_all, axis=0, keepdims=True)
+
+    rho_part = first_sums[0:1, 0:r_cols] + coarse(first_pieces)
+    tz[...] = corner_back(0) + halves_dot(ctt[...], e_scr[...])
+    td[...] = tz[...]
+    xv[...] = jnp.zeros_like(xv)
 
     rho = step = beta = None
     for k in range(ITERS):
         last = k + 1 == ITERS
-        finish_product(k, step, beta)
+        sv[0:NC, :] = sv[0:NC, :] + wcol[...] * td[...]
+        if k == 0:
+            add_jumps(jumps(0, None, None))
         s, d = sv[...], dv[...]
         curve_part = jnp.sum(d * s, axis=0, keepdims=True)
         if not last:
@@ -419,13 +429,14 @@
         dv[...] = z + beta * d
         xv[...] = xv[...] + step * d
         rho = rho_next
-        product(k + 1, k + 2 == ITERS)
+        product(k + 1, k + 2 == ITERS, step, beta)
         tz[...] = tz[...] - step * (tq[...] + corner_back(k + 1))
         td[...] = tz[...] + beta * td[...]
 
-    view = st_buf.at[0, pl.ds(0, n_sub // 2 - 1)]
+    view = st_buf.at[0, pl.ds(0, n_sub // 2 - 1), pl.ds(0, 7)]
     pltpu.make_async_copy(view, view, st_sem.at[0]).wait()
-    pltpu.make_async_copy(st_buf.at[0], st_buf.at[0], st_sem.at[2]).wait()
+    view = st_buf.at[0, :, pl.ds(0, 7)]
+    pltpu.make_async_copy(view, view, st_sem.at[2]).wait()
     for k in range(ITERS + 1):
         drain(p1_buf.at[k], p1_sem.at[k], 0, n_sub, 5 if k < ITERS else 1)
     for k in range(ITERS):
@@ -442,7 +453,7 @@
     n_rows, r = load_cases.shape[2:]
     nz, cm = coarse_basis.shape[2], coarse_inverse.shape[2]
     blk = 8 * n_sub
-    wst = -(-(cm + NC) // 128) * 128
+    wst = max(-(-(cm + NC) // 128) * 128, 4 * NC)
     vec = pltpu.VMEM((n_rows, r), f32)
     vmem = pl.BlockSpec(memory_space=pltpu.VMEM)
     hbm = pl.BlockSpec(memory_space=pltpu.HBM)

time: 76.6 us -> 74.8 us (0.977)
  Pallas kernels: 74.9 us -> 73.1 us
    pallas_call x1, Pallas kernels: 74.9 us -> 73.1 us  [per_device(): pl.pallas_call(functools.partial(kernel, n_sub, n_cl), out_shape=jax.Shap...]
where the time goes in v5:
time: 74.8 us; the launch traced here: 74.7 us
  Pallas kernels  73.1 us (98%)
  local copies, waits for them, and re-layouts  0.89 us (1%)
    pallas_call x1, Pallas kernels, per_device(): pl.pallas_call(functools.partial(kernel, n_sub, n_cl), out_shape=jax.Shap...  73.1 us

profile of v5, /device:TPU:1, one launch (start us, length us, event | category | flops | bytes accessed | tf_op | source)
XLA Modules:
  0.0 74.7 jit_solution(15998332947832360770)
XLA Ops:
  0.7 73.1 %shard_map.91 = f32[1024,64]{1,0:T(8,128)S(1)} custom-call(bf16[1024,1024]{1,0:T(8,128)(2,1)} %bitcast.11, f32[64,1024]{1,0:T(8,128)} %bitcast.12, f32[1,1024]{1,0:T(1,128)} %bitcast.15, f32[6,1,1024]{2,1,0:T(1,128)} %bitcast.13, f32[6,1,192]{2,1,0:T(1,128)} %bitcast.14, f32[1,16]{1,0:T(1,128)} %weight_hbm.1, s32[1,64]{1,0:T(1,128)} %bitcast.16, ...), custom_call_target="tpu_custom_call" | custom-call | tf_op jit(solution)/shard_map/pallas_call | solution.py:467
  73.8 0.9 %copy.10 = f32[1,1,1024,64]{2,3,1,0:T(8,128)} copy(f32[1,1,1024,64]{3,2,1,0:T(8,128)S(1)} %bitcast.10) | data formatting | bytes 524288 | tf_op jit(solution)/shard_map/broadcast_in_dim | solution.py:531

commit v6 on v5

--- a/solution.py
+++ b/solution.py
@@ -410,6 +410,9 @@
             qv[...] = ds + basis_t(e_own)
             send_glue(k + 1, qv)
             tq[...] = scol[...] * td[...] + halves_dot(ctt[...], e_scr[...])
+        else:
+            loads_t[...] = jnp.transpose(xv[...])
+            out_ref[...] = jnp.transpose(dv[...])
         drain(p2_buf.at[k], p2_sem.at[k], 1, n_cl, 2)
         total = jnp.sum(p2_buf[k], axis=0)
         curve = total[0:1, 0:r_cols]
@@ -417,7 +420,9 @@
             rho = total[1:2, r_cols:2 * r_cols]
         step = rho / curve
         if last:
-            out_ref[...] = xv[...] + step * dv[...]
+            same = iota((r_cols, r_cols), 0) == iota((r_cols, r_cols), 1)
+            step = jnp.sum(jnp.where(same, step, 0.0), axis=1, keepdims=True)
+            out_ref[...] = loads_t[...] + step * out_ref[...]
             break
         zs = total[0:1, r_cols:2 * r_cols]
         sq = total[1:2, 0:r_cols]
@@ -466,7 +471,7 @@
     )
     out = pl.pallas_call(
         functools.partial(kernel, n_sub, n_cl),
-        out_shape=jax.ShapeDtypeStruct((n_rows, r), f32),
+        out_shape=jax.ShapeDtypeStruct((r, n_rows), f32),
         in_specs=[hbm] * 9,
         out_specs=vmem,
         scratch_shapes=[
@@ -528,7 +533,7 @@
     )(
         *(pltpu.with_memory_space_constraint(a, pltpu.HBM) for a in operands), glue_link,
     )
-    return out[None, None]
+    return out.T[None, None]
 
 
 def solution(mesh):

time: 74.8 us -> 74.6 us (level)
    broadcast_in_dim x1 -> x0, local copies, waits for them, and re-layouts: 0.89 us -> none  [per_device(): return out[None, None]]
where the time goes in v6:
time: 74.6 us; the launch traced here: 74.4 us
  Pallas kernels  73.1 us (98%)
    pallas_call x1, Pallas kernels, per_device(): pl.pallas_call(functools.partial(kernel, n_sub, n_cl), out_shape=jax.Shap...  73.1 us

profile of v6, /device:TPU:1, one launch (start us, length us, event | category | flops | bytes accessed | tf_op | source)
XLA Modules:
  0.0 74.4 jit_solution(15983854824075271026)
XLA Ops:
  0.7 73.1 %shard_map.91 = f32[64,1024]{1,0:T(8,128)S(1)} custom-call(bf16[1024,1024]{1,0:T(8,128)(2,1)} %bitcast.13, f32[64,1024]{1,0:T(8,128)} %bitcast.14, f32[1,1024]{1,0:T(1,128)} %bitcast.17, f32[6,1,1024]{2,1,0:T(1,128)} %bitcast.15, f32[6,1,192]{2,1,0:T(1,128)} %bitcast.16, f32[1,16]{1,0:T(1,128)} %weight_hbm.1, s32[1,64]{1,0:T(1,128)} %bitcast.18, ...), custom_call_target="tpu_custom_call" | custom-call | tf_op jit(solution)/shard_map/pallas_call | solution.py:472
  73.7 0.7 copy.12
